TPU v7x, 128 devices: a whole 4x4x4 slice. The times are simulated.
128 devices in a mesh: seq: 4 (over y), expert: 32 (over z, x, core).
Axes of the slice: x: 4, y: 4, z: 4, core: 2. Of those that a mesh axis runs over, the one named last changes fastest.
Arguments:
- frames: bfloat16 [16384, 1536], P(('seq', 'expert')), may hold values from -6 to 6
- expert_ids: int32 [16384, 2], P(('seq', 'expert')), may hold values from 0 to 31, all different within a row; in each aligned block of 128 rows (0 to 127, 128 to 255, ...) at most 16 rows name the same one
- gate_weights: float32 [16384, 2], P(('seq', 'expert')), may hold values from 0.2 to 1
- up_weight: bfloat16 [32, 1536, 2048], P('expert'), may hold values from -0.15625 to 0.15625
- down_weight: bfloat16 [32, 2048, 1536], P('expert'), may hold values from -0.125 to 0.125
- smooth_taps: float32 [9, 1536], replicated, may hold values from -0.1 to 0.4
- head_weight: bfloat16 [1536, 527], replicated, may hold values from -0.15625 to 0.15625
- logit_grad: bfloat16 [16384, 527], P(('seq', 'expert')), may hold values from -6 to 6
Outputs:
- logits: bfloat16 [16384, 527], P(('seq', 'expert'))
- frame_grad: bfloat16 [16384, 1536], P(('seq', 'expert'))
- gate_grad: float32 [16384, 2], P(('seq', 'expert'))
Inputs may be any that keep to these rules, and one draw needn't show every extreme that they name: `expert_ids`: the two experts of a frame differ. Among the 256 choices of each aligned block of 128 frames (one device's frames) no expert is named more than 16 times, and in some block some expert is named exactly 16 times.
All inputs are finite; a program needn't handle non-finite values.
Results may differ from a plain program's by a relative error of at most 0.0065.
Values may be sent and summed in bfloat16 or wider, within the bound.
No kernel may reach another device: no remote copies, remote signals or barrier semaphores. Data moves between devices by JAX's collectives and lax.ppermute only.
A program may use at most 128 MiB of HBM per device.

v0:
```python
import jax
import jax.numpy as jnp
from jax import lax
from jax.sharding import PartitionSpec as P

slope_coef = 0.7978845608028654
cubic_coef = 0.044715


def padded_2(block, sides, width):
    for axis, dim in sides:
        count = lax.axis_size(axis)
        forward = [(i, i + 1) for i in range(count - 1)]
        backward = [(target, source) for source, target in forward]
        low = lax.ppermute(
            lax.slice_in_dim(block, block.shape[dim] - width, None, axis=dim), axis, forward
        )
        high = lax.ppermute(lax.slice_in_dim(block, 0, width, axis=dim), axis, backward)
        block = jnp.concatenate([low, block, high], axis=dim)
    return block


def gelu_value(inputs):
    return (
        0.5
        * inputs
        * (1.0 + jnp.tanh(slope_coef * (inputs + cubic_coef * inputs * inputs * inputs)))
    )


def gelu_slope(inputs):
    inner = jnp.tanh(slope_coef * (inputs + cubic_coef * inputs * inputs * inputs))
    return 0.5 * (1.0 + inner) + 0.5 * inputs * (1.0 - inner * inner) * slope_coef * (
        1.0 + 3.0 * cubic_coef * inputs * inputs
    )


def taps_forward(padded, smooth_taps, count):
    summed = jnp.zeros((count, padded.shape[1]), jnp.float32)
    for offset in range(smooth_taps.shape[0]):
        summed = summed + smooth_taps[offset] * padded[offset : offset + count]
    return summed


def taps_backward(padded, smooth_taps, count):
    last_tap = smooth_taps.shape[0] - 1
    summed = jnp.zeros((count, padded.shape[1]), jnp.float32)
    for offset in range(smooth_taps.shape[0]):
        summed = (
            summed + smooth_taps[offset] * padded[last_tap - offset : last_tap - offset + count]
        )
    return summed


def expert_forward(slots_x, up_one, down_one):
    pre = jnp.dot(slots_x, up_one, preferred_element_type=jnp.float32)
    hidden = gelu_value(pre).astype(jnp.bfloat16)
    outputs = jnp.dot(hidden, down_one, preferred_element_type=jnp.float32).astype(jnp.bfloat16)
    return (outputs, pre)


def expert_backward(slots_g, pre, up_one, down_one):
    back_hidden = jnp.einsum("rd,hd->rh", slots_g, down_one, preferred_element_type=jnp.float32)
    pre_grad = (back_hidden * gelu_slope(pre)).astype(jnp.bfloat16)
    return jnp.einsum("rh,dh->rd", pre_grad, up_one, preferred_element_type=jnp.float32).astype(
        jnp.bfloat16
    )


def collect(placing, slots):
    flat_slots = slots.reshape(-1, slots.shape[2])
    return jnp.einsum("sfk,sd->kfd", placing, flat_slots, preferred_element_type=jnp.float32)


def body(
    frames, expert_ids, gate_weights, up_weight, down_weight, smooth_taps, head_weight, logit_grad
):
    owners = lax.axis_size("expert")
    local_rows = frames.shape[0]
    width = frames.shape[1]
    capacity = 4 * local_rows // owners
    margin = smooth_taps.shape[0] // 2
    up_one = up_weight[0]
    down_one = down_weight[0]
    flat_ids = expert_ids.reshape(-1)
    picked = (flat_ids[:, None] == jnp.arange(owners, dtype=jnp.int32)[None, :]).astype(jnp.int32)
    ranks = jnp.sum((jnp.cumsum(picked, axis=0) - 1) * picked, axis=1)
    target = flat_ids * capacity + ranks
    placing = (target[None, :] == jnp.arange(owners * capacity, dtype=jnp.int32)[:, None]).astype(
        jnp.bfloat16
    )
    placing = placing.reshape(owners * capacity, local_rows, 2)
    by_frame = placing[:, :, 0] + placing[:, :, 1]
    send_x = jnp.dot(by_frame, frames, preferred_element_type=jnp.float32).astype(jnp.bfloat16)
    send_x = send_x.reshape(owners, capacity, width)
    smooth_grad = jnp.einsum(
        "fc,dc->fd", logit_grad, head_weight, preferred_element_type=jnp.float32
    ).astype(jnp.bfloat16)
    smooth_grad = lax.optimization_barrier(smooth_grad)
    first_gate = gate_weights[:, 0:1]
    second_gate = gate_weights[:, 1:2]
    received = lax.all_to_all(send_x, "expert", split_axis=0, concat_axis=0, tiled=True)
    layout = received.shape
    outputs, pre = expert_forward(received.reshape(-1, layout[2]), up_one, down_one)
    out_slots = lax.all_to_all(
        outputs.reshape(layout), "expert", split_axis=0, concat_axis=0, tiled=True
    )
    outputs = collect(placing, out_slots)
    mixed = (
        frames.astype(jnp.float32) + first_gate * outputs[0] + second_gate * outputs[1]
    ).astype(jnp.bfloat16)
    mixed = lax.optimization_barrier(mixed)
    joint = jnp.concatenate([mixed, smooth_grad], axis=1)
    joint_padded = padded_2(joint, ((("seq", "expert"), 0),), margin).astype(jnp.float32)
    smooth = taps_forward(joint_padded[:, :width], smooth_taps, local_rows).astype(jnp.bfloat16)
    mixed_grad = taps_backward(joint_padded[:, width:], smooth_taps, local_rows).astype(
        jnp.bfloat16
    )
    mixed_grad = lax.optimization_barrier(mixed_grad)
    send_g = jnp.dot(by_frame, mixed_grad, preferred_element_type=jnp.float32).astype(jnp.bfloat16)
    send_g = send_g.reshape(owners, capacity, width)
    got_x = lax.all_to_all(send_x, "expert", split_axis=0, concat_axis=0, tiled=True)
    got_g = lax.all_to_all(send_g, "expert", split_axis=0, concat_axis=0, tiled=True)
    layout = got_x.shape
    pre = jnp.dot(got_x.reshape(-1, layout[2]), up_one, preferred_element_type=jnp.float32)
    parts = expert_backward(got_g.reshape(-1, layout[2]), pre, up_one, down_one)
    part_slots = lax.all_to_all(
        parts.reshape(layout), "expert", split_axis=0, concat_axis=0, tiled=True
    )
    parts = collect(placing, part_slots)
    logits = jnp.dot(smooth, head_weight, preferred_element_type=jnp.float32).astype(jnp.bfloat16)
    grad_f32 = mixed_grad.astype(jnp.float32)
    frame_grad = (grad_f32 + first_gate * parts[0] + second_gate * parts[1]).astype(jnp.bfloat16)
    gate_grad = jnp.sum(outputs * grad_f32[None, :, :], axis=2).T
    return (logits, frame_grad, gate_grad)


def solution(mesh):
    placed = (
        P(("seq", "expert"), None),
        P(("seq", "expert"), None),
        P(("seq", "expert"), None),
        P("expert", None, None),
        P("expert", None, None),
        P(),
        P(),
        P(("seq", "expert"), None),
    )
    return jax.shard_map(
        body,
        mesh=mesh,
        in_specs=placed,
        out_specs=(
            P(("seq", "expert"), None),
            P(("seq", "expert"), None),
            P(("seq", "expert"), None),
        ),
        check_vma=False,
    )
```

profile of v0, /device:TPU:0, one launch (start us, length us, event | category | flops | bytes accessed | tf_op | source)
XLA Modules:
  0.0 181.8 jit_solution(18104752856146030365)
XLA Ops:
  3.8 1.5 convolution_convert_fusion.1
  5.3 31.2 %all_to_all.21 = bf16[32,16,1536]{2,1,0:T(8,128)(2,1)S(1)} all-to-all(bf16[32,16,1536]{2,1,0:T(8,128)(2,1)S(1)} %bitcast.104), channel_id=1, replica_groups=mesh['seq'=4,'expert'=32] {'expert'}, dimensions={0} | all-to-all | bytes 3145728 | tf_op jit(solution)/shard_map/all_to_all | solution.py:102
  36.5 5.8 %fusion.6 = f32[512,2048]{1,0:T(8,128)S(1)} fusion(bf16[512,1536]{1,0:T(8,128)(2,1)S(1)} %bitcast.109, bf16[1,1536,2048]{2,1,0:T(8,128)(2,1)} %param.11), kind=kOutput, calls=%fused_computation.6 | convolution fusion | flops 3221225472 | bytes 12058624 | tf_op jit(solution)/shard_map/dot_general | solution.py:56
  42.3 4.7 %fusion.20 = bf16[512,1536]{1,0:T(8,128)(2,1)} fusion(bf16[1,2048,1536]{2,1,0:T(8,128)(2,1)S(1)} %bitcast.112, f32[512,2048]{1,0:T(8,128)S(1)} %fusion.6), kind=kOutput, calls=%fused_computation.19 | convolution fusion | flops 3231449088 | bytes 12058624 | tf_op jit(solution)/shard_map/dot_general | solution.py:58
  47.1 4.1 %all-to-all-start.1 = ((bf16[32,16,1536]{2,1,0:T(8,128)(2,1)}), bf16[32,16,1536]{2,1,0:T(8,128)(2,1)S(1)}, u32[]{:S(2)}, u32[]{:S(2)}) async-start(bf16[32,16,1536]{2,1,0:T(8,128)(2,1)} %bitcast.107), calls=%async_computation.1 | async-start | bytes 3145728 | tf_op jit(solution)/shard_map/all_to_all | solution.py:105
  51.2 1.9 %copy.45 = bf16[128,1536]{0,1:T(8,128)(2,1)} copy(bf16[128,1536]{1,0:T(8,128)(2,1)} %param.8) | data formatting | bytes 786432 | tf_op args[0]
  53.1 2.5 %convolution_convert_fusion.2 = bf16[128,1536]{0,1:T(8,128)(2,1)} fusion(bf16[128,527]{0,1:T(8,128)(2,1)} %param.15, bf16[1536,527]{0,1:T(8,128)(2,1)S(1)} %copy-done), kind=kOutput, calls=%fused_computation.24 | convolution fusion | flops 207421440 | bytes 2147072 | tf_op jit(solution)/shard_map/fc,dc->fd/dot_general | solution.py:96
  55.6 19.5 %all-to-all-done.1 = bf16[32,16,1536]{2,1,0:T(8,128)(2,1)S(1)} async-done(((bf16[32,16,1536]{2,1,0:T(8,128)(2,1)}), bf16[32,16,1536]{2,1,0:T(8,128)(2,1)S(1)}, u32[]{:S(2)}, u32[]{:S(2)}) %all-to-all-start.1) | async-done | bytes 1572896 | tf_op jit(solution)/shard_map/all_to_all | solution.py:105
  76.3 2.1 %convolution_bitcast_fusion.1 = f32[2,128,1536]{1,2,0:T(8,128)S(1)} fusion(bf16[512,1536,1]{1,0,2:T(8,128)(2,1)} %bitcast.105, s32[128,2]{0,1:T(2,128)S(1)} %multiply_add_fusion.1), kind=kOutput, calls=%fused_computation.23 | convolution fusion | flops 402784256 | bytes 3146752 | tf_op jit(solution)/shard_map/sfk,sd->kfd/dot_general | solution.py:72
  78.6 1.4 slice_maximum_fusion
  80.0 2.0 %copy.52 = bf16[4,3072]{1,0:T(4,128)(2,1)} copy(bf16[4,3072]{0,1:T(8,128)(2,1)} %get-tuple-element.24) | data formatting | bytes 49152 | tf_op jit(solution)/shard_map/slice | solution.py:16
  82.1 1.9 %collective-permute-start = (bf16[4,3072]{1,0:T(4,128)(2,1)}, bf16[4,3072]{1,0:T(4,128)(2,1)}, u32[]{:S(2)}, u32[]{:S(2)}) collective-permute-start(bf16[4,3072]{1,0:T(4,128)(2,1)} %copy.52), channel_id=1, source_target_pairs={{0,1},{1,2},{2,3},{3,4},{4,5},{5,6},{6,7},{7,8},{8,9},{9,10},{10,1... | collective-permute-start | bytes 73736 | tf_op jit(solution)/shard_map/ppermute | solution.py:15
  83.9 2.0 %copy.53 = bf16[4,3072]{1,0:T(4,128)(2,1)} copy(bf16[4,3072]{0,1:T(8,128)(2,1)} %get-tuple-element.25) | data formatting | bytes 49152 | tf_op jit(solution)/shard_map/slice | solution.py:18
  87.3 1.4 slice_reduce_fusion.9
  88.7 2.0 %copy.54 = bf16[4,3072]{0,1:T(8,128)(2,1)} copy(bf16[4,3072]{1,0:T(4,128)(2,1)} %collective-permute-done) | data formatting | bytes 49152 | tf_op jit(solution)/shard_map/ppermute | solution.py:15
  90.7 2.0 %copy.55 = bf16[4,3072]{0,1:T(8,128)(2,1)} copy(bf16[4,3072]{1,0:T(4,128)(2,1)} %collective-permute-done.1) | data formatting | bytes 49152 | tf_op jit(solution)/shard_map/ppermute | solution.py:18
  92.7 2.5 %maximum_convert_fusion = f32[136,3072]{0,1:T(8,128)S(1)} fusion(bf16[4,3072]{0,1:T(8,128)(2,1)} %copy.55, bf16[128,1536]{0,1:T(8,128)(2,1)} %convolution_convert_fusion.2, bf16[128,1536]{0,1:T(8,128)(2,1)} %copy-done.6, bf16[4,3072]{0,1:T(8,128)(2,1)} %copy.54), kind=kLoop, calls=%fused_computation.29 | loop fusion | flops 3342336 | bytes 2506752 | tf_op jit(solution)/shard_map/convert_element_type | solution.py:114
  95.1 4.0 %fusion.35 = bf16[128,1536]{0,1:T(8,128)(2,1)S(1)} fusion(f32[136,3072]{0,1:T(8,128)S(1)} %maximum_convert_fusion, f32[1536]{0:T(1024)S(1)} %get-tuple-element.22, f32[1536]{0:T(1024)S(1)} %get-tuple-element.23, f32[1536]{0:T(1024)S(1)} %get-tuple-element.16, f32[1536]{0:T(1024)S(1)} %get-tuple-element.17, f32[1536]{0:T(1024)S(1)} %get-tuple-element.18, ...), kind=kLoop, calls=%fused_computation.41 | loop fusion | flops 3538944 | bytes 7526400 | tf_op jit(solution)/shard_map/convert_element_type | solution.py:116
  99.9 35.5 %all_to_all.22 = bf16[32,16,1536]{2,1,0:T(8,128)(2,1)} all-to-all(bf16[32,16,1536]{2,1,0:T(8,128)(2,1)S(1)} %bitcast.103), channel_id=1, replica_groups=mesh['seq'=4,'expert'=32] {'expert'}, dimensions={0} | all-to-all | bytes 3145728 | tf_op jit(solution)/shard_map/all_to_all | solution.py:123
  135.3 14.7 %fusion.17 = bf16[512,1536]{1,0:T(8,128)(2,1)} fusion(bf16[1,1536,2048]{2,1,0:T(8,128)(2,1)} %param.11, f32[512,2048]{1,0:T(8,128)} %copy-done.9, bf16[512,1536]{1,0:T(8,128)(2,1)} %bitcast.108, bf16[1,2048,1536]{2,1,0:T(8,128)(2,1)} %param.12), kind=kOutput, calls=%fused_computation.18 | convolution fusion | flops 6463160320 | bytes 19922944 | tf_op jit(solution)/shard_map/rh,dh->rd/dot_general | solution.py:65
  150.0 4.7 %all-to-all-start.3 = ((bf16[32,16,1536]{2,1,0:T(8,128)(2,1)}), bf16[32,16,1536]{2,1,0:T(8,128)(2,1)}, u32[]{:S(2)}, u32[]{:S(2)}) async-start(bf16[32,16,1536]{2,1,0:T(8,128)(2,1)} %bitcast.106), calls=%async_computation.3 | async-start | bytes 3145728 | tf_op jit(solution)/shard_map/all_to_all | solution.py:127
  156.7 11.2 %convolution_convert_fusion.3 = bf16[128,527]{0,1:T(8,128)(2,1)} fusion(bf16[1536,527]{0,1:T(8,128)(2,1)S(1)} %copy-done, f32[136,3072]{0,1:T(8,128)} %copy-done.1, f32[1536]{0:T(1024)S(1)} %get-tuple-element.22, f32[1536]{0:T(1024)S(1)} %get-tuple-element.23, f32[1536]{0:T(1024)S(1)} %get-tuple-element.16, f32[1536]{0:T(1024)S(1)} %get-tuple-element.17, ...), kind=kOutput, calls=%fused_computation.31 | convolution fusion | flops 210831232 | bytes 8887040 | tf_op jit(solution)/shard_map/dot_general | solution.py:131
  167.9 10.8 %all-to-all-done.3 = bf16[32,16,1536]{2,1,0:T(8,128)(2,1)} async-done(((bf16[32,16,1536]{2,1,0:T(8,128)(2,1)}), bf16[32,16,1536]{2,1,0:T(8,128)(2,1)}, u32[]{:S(2)}, u32[]{:S(2)}) %all-to-all-start.3) | async-done | bytes 1572896 | tf_op jit(solution)/shard_map/all_to_all | solution.py:127
  178.6 2.0 %convolution_bitcast_fusion = f32[2,128,1536]{1,2,0:T(8,128)S(1)} fusion(bf16[512,1536,1]{1,0,2:T(8,128)(2,1)} %bitcast.19, s32[128,2]{0,1:T(2,128)S(1)} %multiply_add_fusion.1), kind=kOutput, calls=%fused_computation.22 | convolution fusion | flops 402784256 | bytes 3146752 | tf_op jit(solution)/shard_map/sfk,sd->kfd/dot_general | solution.py:72
  (48 shorter events, 9.5 us)
Async XLA Ops:
  0.6 52.5 %copy-start = (bf16[1536,527]{0,1:T(8,128)(2,1)S(1)}, bf16[1536,527]{0,1:T(8,128)(2,1)}, u32[]{:S(2)}) copy-start(bf16[1536,527]{0,1:T(8,128)(2,1)} %param.14) | copy-start | bytes 4856836
  5.3 37.0 %slice-start = ((s8[6291456]{0:T(1024)(128)(4,1)}), s8[4194304]{0:T(1024)(128)(4,1)S(1)}, s32[]{:S(2)}) async-start(s8[6291456]{0:T(1024)(128)(4,1)} %bitcast.111), calls=%async_computation.4 | async-start | bytes 8388608
  36.5 5.8 %slice-start.1 = ((s8[6291456]{0:T(1024)(128)(4,1)}), s8[2097152]{0:T(1024)(128)(4,1)S(1)}, s32[]{:S(2)}) async-start(s8[6291456]{0:T(1024)(128)(4,1)} %bitcast.111), calls=%async_computation.5 | async-start | bytes 4194304
  42.3 4.8 %copy-start.9 = (f32[512,2048]{1,0:T(8,128)}, f32[512,2048]{1,0:T(8,128)S(1)}, u32[]{:S(2)}) copy-start(f32[512,2048]{1,0:T(8,128)S(1)} %fusion.6) | copy-start | bytes 12582916
  47.1 8.5 %copy-start.8 = (f32[128,2]{0,1:T(2,128)S(1)}, f32[128,2]{0,1:T(2,128)}, u32[]{:S(2)}) copy-start(f32[128,2]{0,1:T(2,128)} %param.10) | copy-start | bytes 3076
  47.1 28.0 %all-to-all-start.1 = ((bf16[32,16,1536]{2,1,0:T(8,128)(2,1)}), bf16[32,16,1536]{2,1,0:T(8,128)(2,1)S(1)}, u32[]{:S(2)}, u32[]{:S(2)}) async-start(bf16[32,16,1536]{2,1,0:T(8,128)(2,1)} %bitcast.107), calls=%async_computation.1 | async-start | bytes 3145728 | tf_op jit(solution)/shard_map/all_to_all | solution.py:105
  75.1 1.2 copy-start.4
  76.3 2.1 %copy-start.7 = (bf16[128,1536]{0,1:T(8,128)(2,1)S(1)}, bf16[128,1536]{0,1:T(8,128)(2,1)}, u32[]{:S(2)}) copy-start(bf16[128,1536]{0,1:T(8,128)(2,1)} %copy.45) | copy-start | bytes 1179652
  76.3 2.3 %copy-start.5 = (bf16[128,1536]{0,1:T(8,128)(2,1)S(1)}, bf16[128,1536]{0,1:T(8,128)(2,1)}, u32[]{:S(2)}) copy-start(bf16[128,1536]{0,1:T(8,128)(2,1)} %convolution_convert_fusion.2) | copy-start | bytes 1179652
  78.6 1.5 copy-start.6
  82.1 6.6 %collective-permute-start = (bf16[4,3072]{1,0:T(4,128)(2,1)}, bf16[4,3072]{1,0:T(4,128)(2,1)}, u32[]{:S(2)}, u32[]{:S(2)}) collective-permute-start(bf16[4,3072]{1,0:T(4,128)(2,1)} %copy.52), channel_id=1, source_target_pairs={{0,1},{1,2},{2,3},{3,4},{4,5},{5,6},{6,7},{7,8},{8,9},{9,10},{10,1... | collective-permute-start | bytes 73736 | tf_op jit(solution)/shard_map/ppermute | solution.py:15
  86.0 4.7 %collective-permute-start.1 = (bf16[4,3072]{1,0:T(4,128)(2,1)}, bf16[4,3072]{1,0:T(4,128)(2,1)}, u32[]{:S(2)}, u32[]{:S(2)}) collective-permute-start(bf16[4,3072]{1,0:T(4,128)(2,1)} %copy.53), channel_id=1, source_target_pairs={{1,0},{2,1},{3,2},{4,3},{5,4},{6,5},{7,6},{8,7},{9,8},{10,9},{11,1... | collective-permute-start | bytes 73736 | tf_op jit(solution)/shard_map/ppermute | solution.py:18
  95.1 4.0 %copy-start.1 = (f32[136,3072]{0,1:T(8,128)}, f32[136,3072]{0,1:T(8,128)S(1)}, u32[]{:S(2)}) copy-start(f32[136,3072]{0,1:T(8,128)S(1)} %maximum_convert_fusion) | copy-start | bytes 5013508
  99.1 0.7 copy-start.2
  150.0 28.6 %all-to-all-start.3 = ((bf16[32,16,1536]{2,1,0:T(8,128)(2,1)}), bf16[32,16,1536]{2,1,0:T(8,128)(2,1)}, u32[]{:S(2)}, u32[]{:S(2)}) async-start(bf16[32,16,1536]{2,1,0:T(8,128)(2,1)} %bitcast.106), calls=%async_computation.3 | async-start | bytes 3145728 | tf_op jit(solution)/shard_map/all_to_all | solution.py:127
  167.9 12.8 %copy-start.3 = (bf16[128,1536]{0,1:T(8,128)(2,1)S(1)}, bf16[128,1536]{0,1:T(8,128)(2,1)}, u32[]{:S(2)}) copy-start(bf16[128,1536]{0,1:T(8,128)(2,1)} %copy-done.2) | copy-start | bytes 1179652
where the time goes:
time: 183 us; the launch traced here: 182 us
  blocking collectives  66.6 us (36%)
  matrix products  45.1 us (25%)
  waiting for transfers between devices  30.3 us (17%)
  local copies, waits for them, and re-layouts  15.2 us (8%)
  starting transfers between devices  12 us (7%)
  other arithmetic  11.6 us (6%)
    all_to_all x1, blocking collectives, body(): lax.all_to_all(send_g, 'expert', split_axis=0, concat_axis=0, tiled=True)  35.5 us
    all_to_all x1, blocking collectives, body(): lax.all_to_all(send_x, 'expert', split_axis=0, concat_axis=0, tiled=True)  31.2 us
    all_to_all x1, waiting for transfers between devices, body(): lax.all_to_all(outputs.reshape(layout), 'expert', split_axis=0, concat_ax...  19.5 us
    dot_general x1, matrix products, expert_backward(): jnp.einsum('rh,dh->rd', pre_grad, up_one, preferred_element_type=jnp.floa...  14.7 us
    dot_general x1, matrix products, body(): jnp.dot(smooth, head_weight, preferred_element_type=jnp.float32)  11.2 us
    all_to_all x1, waiting for transfers between devices, body(): lax.all_to_all(parts.reshape(layout), 'expert', split_axis=0, concat_axis...  10.8 us
    dot_general x1, matrix products, expert_forward(): pre = jnp.dot(slots_x, up_one, preferred_element_type=jnp.float32)  5.77 us
    unnamed x27, local copies, waits for them, and re-layouts  5.13 us
  transfers between devices with their start and end apart: 4, of which 2 were waited for; matrix products, arithmetic and copies ran while one was open for 13% of the time, Pallas kernels for 0%

commit v1 on v0

v1 whole, which is shorter than its diff:
```python
import functools

import jax
import jax.numpy as jnp
from jax import lax
from jax.experimental import pallas as pl
from jax.experimental.pallas import tpu as pltpu
from jax.sharding import PartitionSpec as P

slope_coef = 0.7978845608028654
cubic_coef = 0.044715
bf16 = jnp.bfloat16
f32 = jnp.float32
i32 = jnp.int32


def gelu_value(inputs):
    return (
        0.5
        * inputs
        * (1.0 + jnp.tanh(slope_coef * (inputs + cubic_coef * inputs * inputs * inputs)))
    )


def gelu_slope(inputs):
    inner = jnp.tanh(slope_coef * (inputs + cubic_coef * inputs * inputs * inputs))
    return 0.5 * (1.0 + inner) + 0.5 * inputs * (1.0 - inner * inner) * slope_coef * (
        1.0 + 3.0 * cubic_coef * inputs * inputs
    )


def cost(flops, moved):
    return pl.CostEstimate(flops=flops, bytes_accessed=moved, transcendentals=0)


def whole(shape):
    return pl.BlockSpec(shape, lambda j: (0,) * len(shape))


def cols(rows, tile):
    return pl.BlockSpec((rows, tile), lambda j: (0, j))


def iota(shape, dim):
    return lax.broadcasted_iota(i32, shape, dim)


def to_column(row):
    n = row.shape[1]
    diagonal = iota((n, n), 0) == iota((n, n), 1)
    return jnp.sum(jnp.where(diagonal, row, jnp.zeros_like(row)), axis=1, keepdims=True)


def to_row(column):
    n = column.shape[0]
    diagonal = iota((n, n), 0) == iota((n, n), 1)
    return jnp.sum(jnp.where(diagonal, column, jnp.zeros_like(column)), axis=0, keepdims=True)


def send_mask(target, slots):
    rows = iota((slots, target.shape[1]), 0)
    hit = (rows == target[0:1, :]) | (rows == target[1:2, :])
    return jnp.where(hit, 1.0, 0.0).astype(bf16)


def pick_mask(target_row, slots):
    column = to_column(target_row)
    return jnp.where(iota((column.shape[0], slots), 1) == column, 1.0, 0.0).astype(bf16)


def fill_padded(padded, low, block, high):
    rows = block.shape[0]
    margin = low.shape[0]
    padded[8 - margin : 8, :] = low.astype(f32)
    padded[8 : 8 + rows, :] = block.astype(f32)
    padded[8 + rows : 8 + rows + margin, :] = high.astype(f32)


def dispatch_kernel(owners, capacity, ids_ref, frames_ref, send_ref, target_ref, mask_ref):
    slots = owners * capacity
    count = ids_ref.shape[1]

    @pl.when(pl.program_id(0) == 0)
    def _():
        ids = ids_ref[...]
        first, second = ids[0:1, :], ids[1:2, :]
        experts = iota((owners, count), 0)
        first_hot = jnp.where(experts == first, 1.0, 0.0)
        second_hot = jnp.where(experts == second, 1.0, 0.0)
        before = jnp.where(iota((count, count), 0) < iota((count, count), 1), 1.0, 0.0).astype(bf16)
        first_seen = jnp.dot(first_hot.astype(bf16), before, preferred_element_type=f32)
        second_seen = jnp.dot(second_hot.astype(bf16), before, preferred_element_type=f32)
        second_seen = second_seen + jnp.sum(first_hot, axis=1, keepdims=True)
        first_rank = jnp.sum(first_seen * first_hot, axis=0, keepdims=True).astype(i32)
        second_rank = jnp.sum(second_seen * second_hot, axis=0, keepdims=True).astype(i32)
        target = jnp.concatenate(
            [first * capacity + first_rank, second * capacity + second_rank], axis=0
        )
        target_ref[...] = target
        mask_ref[...] = send_mask(target, slots)

    send_ref[...] = jnp.dot(
        mask_ref[...], frames_ref[...], preferred_element_type=f32
    ).astype(bf16)


def dispatch(ids, frames, owners, capacity, tile=512):
    rows, width = frames.shape
    slots = owners * capacity

    return pl.pallas_call(
        functools.partial(dispatch_kernel, owners, capacity),
        grid=(width // tile,),
        out_shape=(
            jax.ShapeDtypeStruct((slots, width), bf16),
            jax.ShapeDtypeStruct((2, rows), i32),
        ),
        in_specs=[whole((2, rows)), cols(rows, tile)],
        out_specs=(cols(slots, tile), whole((2, rows))),
        scratch_shapes=[pltpu.VMEM((slots, rows), bf16)],
        cost_estimate=cost(2 * slots * rows * width, 2 * (slots + rows) * width),
        name="dispatch",
    )(ids, frames)


def grad_kernel(target_ref, low_ref, block_ref, high_ref, taps_ref, grad_ref, send_ref, mask_ref, padded):
    rows = block_ref.shape[0]
    taps = taps_ref.shape[0]

    @pl.when(pl.program_id(0) == 0)
    def _():
        mask_ref[...] = send_mask(target_ref[...], mask_ref.shape[0])

    fill_padded(padded, low_ref[...], block_ref[...], high_ref[...])
    summed = jnp.zeros(block_ref.shape, f32)
    for offset in range(taps):
        start = 8 - taps // 2 + taps - 1 - offset
        summed = summed + taps_ref[offset : offset + 1, :] * padded[start : start + rows, :]
    grad = summed.astype(bf16)
    grad_ref[...] = grad
    send_ref[...] = jnp.dot(mask_ref[...], grad, preferred_element_type=f32).astype(bf16)


def grad_dispatch(target, low, block, high, taps, slots, tile=512):
    rows, width = block.shape
    margin = low.shape[0]
    return pl.pallas_call(
        grad_kernel,
        grid=(width // tile,),
        out_shape=(
            jax.ShapeDtypeStruct((rows, width), bf16),
            jax.ShapeDtypeStruct((slots, width), bf16),
        ),
        in_specs=[
            whole((2, rows)),
            cols(margin, tile),
            cols(rows, tile),
            cols(margin, tile),
            cols(taps.shape[0], tile),
        ],
        out_specs=(cols(rows, tile), cols(slots, tile)),
        scratch_shapes=[pltpu.VMEM((slots, rows), bf16), pltpu.VMEM((rows + 16, tile), f32)],
        cost_estimate=cost(2 * slots * rows * width, 2 * (slots + 2 * rows) * width),
        name="grad_dispatch",
    )(target, low, block, high, taps)


def mix_kernel(
    target_ref, gates_ref, slots_ref, frames_ref, grad_ref, mixed_ref, gate_grad_ref,
    first_mask, second_mask, gate_columns, sums,
):
    step = pl.program_id(0)

    @pl.when(step == 0)
    def _():
        target = target_ref[...]
        gates = gates_ref[...]
        first_mask[...] = pick_mask(target[0:1, :], first_mask.shape[1])
        second_mask[...] = pick_mask(target[1:2, :], second_mask.shape[1])
        gate_columns[:, 0:1] = to_column(gates[0:1, :])
        gate_columns[:, 1:2] = to_column(gates[1:2, :])
        sums[...] = jnp.zeros_like(sums)

    slots = slots_ref[...]
    grad = grad_ref[...].astype(f32)
    first = jnp.dot(first_mask[...], slots, preferred_element_type=f32)
    second = jnp.dot(second_mask[...], slots, preferred_element_type=f32)
    mixed = frames_ref[...].astype(f32) + gate_columns[:, 0:1] * first
    mixed_ref[...] = (mixed + gate_columns[:, 1:2] * second).astype(bf16)
    sums[:, 0:1] += jnp.sum(first * grad, axis=1, keepdims=True)
    sums[:, 1:2] += jnp.sum(second * grad, axis=1, keepdims=True)

    @pl.when(step == pl.num_programs(0) - 1)
    def _():
        gate_grad_ref[0:1, :] = to_row(sums[:, 0:1])
        gate_grad_ref[1:2, :] = to_row(sums[:, 1:2])


def mix(target, gates, slots, frames, grad, tile=512):
    rows, width = frames.shape
    n = slots.shape[0]
    return pl.pallas_call(
        mix_kernel,
        grid=(width // tile,),
        out_shape=(
            jax.ShapeDtypeStruct((rows, width), bf16),
            jax.ShapeDtypeStruct((2, rows), f32),
        ),
        in_specs=[
            whole((2, rows)),
            whole((2, rows)),
            cols(n, tile),
            cols(rows, tile),
            cols(rows, tile),
        ],
        out_specs=(cols(rows, tile), whole((2, rows))),
        scratch_shapes=[
            pltpu.VMEM((rows, n), bf16),
            pltpu.VMEM((rows, n), bf16),
            pltpu.VMEM((rows, 2), f32),
            pltpu.VMEM((rows, 2), f32),
        ],
        cost_estimate=cost(4 * n * rows * width, 2 * (n + 3 * rows) * width),
        name="mix",
    )(target, gates, slots, frames, grad)


def head_kernel(low_ref, block_ref, high_ref, taps_ref, head_ref, logits_ref, padded):
    rows, width = block_ref.shape
    taps = taps_ref.shape[0]
    fill_padded(padded, low_ref[...], block_ref[...], high_ref[...])
    summed = jnp.zeros(block_ref.shape, f32)
    for offset in range(taps):
        start = 8 - taps // 2 + offset
        summed = summed + taps_ref[offset : offset + 1, :] * padded[start : start + rows, :]
    logits_ref[...] += lax.dot_general(
        head_ref[...], summed.astype(bf16), (((1,), (1,)), ((), ())), preferred_element_type=f32
    )


def head_step(low_ref, block_ref, high_ref, taps_ref, head_ref, logits_ref, padded, total):
    step = pl.program_id(0)

    @pl.when(step == 0)
    def _():
        total[...] = jnp.zeros_like(total)

    head_kernel(low_ref, block_ref, high_ref, taps_ref, head_ref, total, padded)

    @pl.when(step == pl.num_programs(0) - 1)
    def _():
        logits_ref[...] = total[...].astype(bf16)


def head(low, block, high, taps, head_t, tile=512):
    rows, width = block.shape
    margin = low.shape[0]
    classes = head_t.shape[0]
    return pl.pallas_call(
        head_step,
        grid=(width // tile,),
        out_shape=jax.ShapeDtypeStruct((classes, rows), bf16),
        in_specs=[
            cols(margin, tile),
            cols(rows, tile),
            cols(margin, tile),
            cols(taps.shape[0], tile),
            cols(classes, tile),
        ],
        out_specs=whole((classes, rows)),
        scratch_shapes=[
            pltpu.VMEM((rows + 16, tile), f32),
            pltpu.VMEM((classes, rows), f32),
        ],
        cost_estimate=cost(2 * classes * rows * width, 2 * (classes + rows) * width),
        name="head",
    )(low, block, high, taps, head_t)


def finish_kernel(
    target_ref, gates_ref, slots_ref, grad_ref, out_ref, first_mask, second_mask, gate_columns
):
    @pl.when(pl.program_id(0) == 0)
    def _():
        target = target_ref[...]
        gates = gates_ref[...]
        first_mask[...] = pick_mask(target[0:1, :], first_mask.shape[1])
        second_mask[...] = pick_mask(target[1:2, :], second_mask.shape[1])
        gate_columns[:, 0:1] = to_column(gates[0:1, :])
        gate_columns[:, 1:2] = to_column(gates[1:2, :])

    slots = slots_ref[...]
    first = jnp.dot(first_mask[...], slots, preferred_element_type=f32)
    second = jnp.dot(second_mask[...], slots, preferred_element_type=f32)
    total = grad_ref[...].astype(f32) + gate_columns[:, 0:1] * first
    out_ref[...] = (total + gate_columns[:, 1:2] * second).astype(bf16)


def finish(target, gates, slots, grad, tile=512):
    rows, width = grad.shape
    n = slots.shape[0]
    return pl.pallas_call(
        finish_kernel,
        grid=(width // tile,),
        out_shape=jax.ShapeDtypeStruct((rows, width), bf16),
        in_specs=[whole((2, rows)), whole((2, rows)), cols(n, tile), cols(rows, tile)],
        out_specs=cols(rows, tile),
        scratch_shapes=[
            pltpu.VMEM((rows, n), bf16),
            pltpu.VMEM((rows, n), bf16),
            pltpu.VMEM((rows, 2), f32),
        ],
        cost_estimate=cost(4 * n * rows * width, 2 * (n + 2 * rows) * width),
        name="finish",
    )(target, gates, slots, grad)


def edges(block, width):
    axes = ("seq", "expert")
    count = lax.axis_size(axes)
    forward = [(i, i + 1) for i in range(count - 1)]
    backward = [(target, source) for source, target in forward]
    low = lax.ppermute(block[block.shape[0] - width :], axes, forward)
    high = lax.ppermute(block[:width], axes, backward)
    return low, high


def exchange(slots, owners):
    blocks = slots.reshape(owners, -1, slots.shape[1])
    blocks = lax.all_to_all(blocks, "expert", split_axis=0, concat_axis=0, tiled=True)
    return blocks.reshape(slots.shape)


def body(
    frames, expert_ids, gate_weights, up_weight, down_weight, smooth_taps, head_weight, logit_grad
):
    owners = lax.axis_size("expert")
    local_rows = frames.shape[0]
    capacity = 4 * local_rows // owners
    slots = owners * capacity
    margin = smooth_taps.shape[0] // 2
    up_one = up_weight[0]
    down_one = down_weight[0]
    gates = gate_weights.T
    head_t = head_weight.T

    send_x, target = dispatch(expert_ids.T, frames, owners, capacity)
    got_x = exchange(send_x, owners)

    smooth_grad = jnp.einsum(
        "fc,dc->fd", logit_grad, head_weight, preferred_element_type=f32
    ).astype(bf16)
    smooth_grad = lax.optimization_barrier(smooth_grad)
    low, high = edges(smooth_grad, margin)
    mixed_grad, send_g = grad_dispatch(target, low, smooth_grad, high, smooth_taps, slots)
    got_g = exchange(send_g, owners)

    pre = jnp.dot(got_x, up_one, preferred_element_type=f32)
    hidden = gelu_value(pre).astype(bf16)
    outputs = jnp.dot(hidden, down_one, preferred_element_type=f32).astype(bf16)
    out_slots = exchange(outputs, owners)

    back_hidden = jnp.einsum("rd,hd->rh", got_g, down_one, preferred_element_type=f32)
    pre_grad = (back_hidden * gelu_slope(pre)).astype(bf16)
    parts = jnp.einsum("rh,dh->rd", pre_grad, up_one, preferred_element_type=f32).astype(bf16)
    part_slots = exchange(parts, owners)

    mixed, gate_grad = mix(target, gates, out_slots, frames, mixed_grad)
    low, high = edges(mixed, margin)
    logits = head(low, mixed, high, smooth_taps, head_t)
    frame_grad = finish(target, gates, part_slots, mixed_grad)
    return (logits.T, frame_grad, gate_grad.T)


def solution(mesh):
    placed = (
        P(("seq", "expert"), None),
        P(("seq", "expert"), None),
        P(("seq", "expert"), None),
        P("expert", None, None),
        P("expert", None, None),
        P(),
        P(),
        P(("seq", "expert"), None),
    )
    return jax.shard_map(
        body,
        mesh=mesh,
        in_specs=placed,
        out_specs=(
            P(("seq", "expert"), None),
            P(("seq", "expert"), None),
            P(("seq", "expert"), None),
        ),
        check_vma=False,
    )
```

time: 183 us -> 135 us (0.74)
  blocking collectives: 66.6 us -> 0 us
  starting transfers between devices: 12 us -> 32.2 us
  Pallas kernels: 0 us -> 20 us
  matrix products: 45.1 us -> 28.4 us
  waiting for transfers between devices: 30.3 us -> 46.1 us
  other arithmetic: 11.6 us -> 0 us
  local copies, waits for them, and re-layouts: 15.2 us -> 7.07 us
    all_to_all x2 -> x0, blocking collectives: 66.6 us -> none  [the longest x1 35.5 us: body(): lax.all_to_all(send_g, 'expert', split_axis=0, concat_axis=0, tiled=True)]
    pallas_call x0 -> x5, Pallas kernels: none -> 20 us  [the longest x1 4.23 us: head(): pl.pallas_call(head_step, grid=(width // tile,), out_shape=jax.ShapeDtype...]
    dot_general x9 -> x4, matrix products: 45.1 us -> 28.4 us  [the longest x1 14.7 us: body(): jnp.einsum('rh,dh->rd', pre_grad, up_one, preferred_element_type=f32)]
    all_to_all x2 -> x4, waiting for transfers between devices: 30.3 us -> 45.3 us  [exchange(): lax.all_to_all(blocks, 'expert', split_axis=0, concat_axis=0, tiled=True)]
    all_to_all x2 -> x4, starting transfers between devices: 8.81 us -> 23.5 us  [exchange(): lax.all_to_all(blocks, 'expert', split_axis=0, concat_axis=0, tiled=True)]
    convert_element_type x7 -> x0, other arithmetic: 7.87 us -> none  [the longest x1 3.97 us: body(): taps_backward(joint_padded[:, width:], smooth_taps, local_rows)]
    ppermute x2 -> x4, starting transfers between devices: 3.16 us -> 8.65 us  [the longest x2 6.06 us: edges(): low = lax.ppermute(block[block.shape[0] - width:], axes, forward)]
    slice x4 -> x2, local copies, waits for them, and re-layouts: 5.69 us -> 0.78 us  [edges(): high = lax.ppermute(block[:width], axes, backward)]
  transfers between devices with their start and end apart: 4 -> 8, of which waited for: 2 -> 5; matrix products, arithmetic and copies ran while one was open for 13% -> 22% of each run, Pallas kernels for 0% -> 9%
where the time goes in v1:
time: 135 us
  waiting for transfers between devices  46.1 us (34%)
  starting transfers between devices  32.2 us (24%)
  matrix products  28.4 us (21%)
  Pallas kernels  20 us (15%)
  local copies, waits for them, and re-layouts  7.07 us (5%)
    all_to_all x4, waiting for transfers between devices, exchange(): lax.all_to_all(blocks, 'expert', split_axis=0, concat_axis=0, tiled=True)  45.3 us
    all_to_all x4, starting transfers between devices, exchange(): lax.all_to_all(blocks, 'expert', split_axis=0, concat_axis=0, tiled=True)  23.5 us
    dot_general x1, matrix products, body(): jnp.einsum('rh,dh->rd', pre_grad, up_one, preferred_element_type=f32)  14.7 us
    dot_general x1, matrix products, body(): outputs = jnp.dot(hidden, down_one, preferred_element_type=f32).astype(bf16)  7.63 us
    unnamed x22, local copies, waits for them, and re-layouts  6.28 us
    ppermute x2, starting transfers between devices, edges(): low = lax.ppermute(block[block.shape[0] - width:], axes, forward)  6.06 us
    dot_general x1, matrix products, body(): pre = jnp.dot(got_x, up_one, preferred_element_type=f32)  5.63 us
    pallas_call x1, Pallas kernels, head(): pl.pallas_call(head_step, grid=(width // tile,), out_shape=jax.ShapeDtype...  4.23 us
  transfers between devices with their start and end apart: 8, of which 5 were waited for; matrix products, arithmetic and copies ran while one was open for 22% of the time, Pallas kernels for 9%

profile of v1, /device:TPU:0, one launch (start us, length us, event | category | flops | bytes accessed | tf_op | source)
XLA Modules:
  0.0 134.5 jit_solution(8421843641293970041)
XLA Ops:
  0.7 3.8 %dispatch.1 = (bf16[512,1536]{1,0:T(8,128)(2,1)}, s32[2,128]{1,0:T(2,128)}) custom-call(s32[2,128]{1,0:T(2,128)} %bitcast.46, bf16[128,1536]{1,0:T(8,128)(2,1)} %frames_ref.3), custom_call_target="tpu_custom_call" | custom-call | flops 201326592 | bytes 1966080 | tf_op jit(solution)/shard_map/dispatch/pallas_call | solution.py:111
  4.4 8.3 %all-to-all-start = ((bf16[32,16,1536]{2,1,0:T(8,128)(2,1)}), bf16[32,16,1536]{2,1,0:T(8,128)(2,1)S(1)}, u32[]{:S(2)}, u32[]{:S(2)}) async-start(bf16[32,16,1536]{2,1,0:T(8,128)(2,1)} %bitcast.39), calls=%async_computation | async-start | bytes 3145728 | tf_op jit(solution)/shard_map/all_to_all | solution.py:330
  14.0 1.3 collective-permute-start.1
  15.3 3.0 %collective-permute-start = (bf16[4,1536]{1,0:T(4,128)(2,1)S(1)}, bf16[4,1536]{1,0:T(4,128)(2,1)S(1)}, u32[]{:S(2)}, u32[]{:S(2)}) collective-permute-start(bf16[4,1536]{1,0:T(4,128)(2,1)S(1)} %get-tuple-element.18), channel_id=1, source_target_pairs={{0,1},{1,2},{2,3},{3,4},{4,5},{5,6},{6,7},{7,8},{8,9},{9,10},{10,1... | collective-permute-start | bytes 36872 | tf_op jit(solution)/shard_map/ppermute | solution.py:323
  18.4 0.8 collective-permute-done.low_ref
  19.8 4.2 %grad_dispatch.1 = (bf16[128,1536]{1,0:T(8,128)(2,1)}, bf16[512,1536]{1,0:T(8,128)(2,1)}) custom-call(s32[2,128]{1,0:T(2,128)} %get-tuple-element.9.target_ref, bf16[4,1536]{1,0:T(4,128)(2,1)} %copy-done.9, bf16[128,1536]{1,0:T(8,128)(2,1)} %copy-done.5, bf16[4,1536]{1,0:T(4,128)(2,1)} %copy-done.8, f32[9,1536]{1,0:T(8,128)} %taps_ref.3), custom_call_target="tpu_custom_call" | custom-call | flops 201326592 | bytes 2359296 | tf_op jit(solution)/shard_map/grad_dispatch/pallas_call | solution.py:147
  23.9 12.7 %all-to-all-done = bf16[32,16,1536]{2,1,0:T(8,128)(2,1)S(1)} async-done(((bf16[32,16,1536]{2,1,0:T(8,128)(2,1)}), bf16[32,16,1536]{2,1,0:T(8,128)(2,1)S(1)}, u32[]{:S(2)}, u32[]{:S(2)}) %all-to-all-start) | async-done | bytes 1572896 | tf_op jit(solution)/shard_map/all_to_all | solution.py:330
  36.6 7.3 %all-to-all-start.2 = ((bf16[32,16,1536]{2,1,0:T(8,128)(2,1)}), bf16[32,16,1536]{2,1,0:T(8,128)(2,1)S(1)}, u32[]{:S(2)}, u32[]{:S(2)}) async-start(bf16[32,16,1536]{2,1,0:T(8,128)(2,1)} %bitcast.41), calls=%async_computation.2 | async-start | bytes 3145728 | tf_op jit(solution)/shard_map/all_to_all | solution.py:330
  43.9 5.6 %fusion.6 = f32[512,2048]{1,0:T(8,128)S(1)} fusion(bf16[512,1536]{1,0:T(8,128)(2,1)S(1)} %bitcast.38, bf16[1,1536,2048]{2,1,0:T(8,128)(2,1)} %param.11), kind=kOutput, calls=%fused_computation.6 | convolution fusion | flops 3221225472 | bytes 12058624 | tf_op jit(solution)/shard_map/dot_general | solution.py:358
  49.6 1.9 %copy-done.10 = f32[512,2048]{1,0:T(8,128)} copy-done((f32[512,2048]{1,0:T(8,128)}, f32[512,2048]{1,0:T(8,128)S(1)}, u32[]{:S(2)}) %copy-start.10) | copy-done | bytes 4194328
  51.5 7.6 %fusion.20 = bf16[512,1536]{1,0:T(8,128)(2,1)} fusion(bf16[1,2048,1536]{2,1,0:T(8,128)(2,1)} %param.12, f32[512,2048]{1,0:T(8,128)S(1)} %fusion.6), kind=kOutput, calls=%fused_computation.19 | convolution fusion | flops 3231449088 | bytes 12058624 | tf_op jit(solution)/shard_map/dot_general | solution.py:360
  59.1 8.7 %all-to-all-done.2 = bf16[32,16,1536]{2,1,0:T(8,128)(2,1)S(1)} async-done(((bf16[32,16,1536]{2,1,0:T(8,128)(2,1)}), bf16[32,16,1536]{2,1,0:T(8,128)(2,1)S(1)}, u32[]{:S(2)}, u32[]{:S(2)}) %all-to-all-start.2) | async-done | bytes 1572896 | tf_op jit(solution)/shard_map/all_to_all | solution.py:330
  67.8 1.2 copy-done.4
  69.1 4.0 %all-to-all-start.1 = ((bf16[32,16,1536]{2,1,0:T(8,128)(2,1)}), bf16[32,16,1536]{2,1,0:T(8,128)(2,1)S(1)}, u32[]{:S(2)}, u32[]{:S(2)}) async-start(bf16[32,16,1536]{2,1,0:T(8,128)(2,1)} %bitcast.6), calls=%async_computation.1 | async-start | bytes 3145728 | tf_op jit(solution)/shard_map/all_to_all | solution.py:330
  73.0 14.7 %fusion.17 = bf16[512,1536]{1,0:T(8,128)(2,1)} fusion(bf16[1,1536,2048]{2,1,0:T(8,128)(2,1)} %param.11, f32[512,2048]{1,0:T(8,128)} %copy-done.10, bf16[512,1536]{1,0:T(8,128)(2,1)} %bitcast.42, bf16[1,2048,1536]{2,1,0:T(8,128)(2,1)} %param.12), kind=kOutput, calls=%fused_computation.18 | convolution fusion | flops 6463160320 | bytes 19922944 | tf_op jit(solution)/shard_map/rh,dh->rd/dot_general | solution.py:365
  87.7 9.2 %all-to-all-done.1 = bf16[32,16,1536]{2,1,0:T(8,128)(2,1)S(1)} async-done(((bf16[32,16,1536]{2,1,0:T(8,128)(2,1)}), bf16[32,16,1536]{2,1,0:T(8,128)(2,1)S(1)}, u32[]{:S(2)}, u32[]{:S(2)}) %all-to-all-start.1) | async-done | bytes 1572896 | tf_op jit(solution)/shard_map/all_to_all | solution.py:330
  96.9 4.0 %all-to-all-start.3 = ((bf16[32,16,1536]{2,1,0:T(8,128)(2,1)}), bf16[32,16,1536]{2,1,0:T(8,128)(2,1)S(1)}, u32[]{:S(2)}, u32[]{:S(2)}) async-start(bf16[32,16,1536]{2,1,0:T(8,128)(2,1)} %bitcast.40), calls=%async_computation.3 | async-start | bytes 3145728 | tf_op jit(solution)/shard_map/all_to_all | solution.py:330
  100.9 4.1 %mix.1 = (bf16[128,1536]{1,0:T(8,128)(2,1)}, f32[2,128]{1,0:T(2,128)}) custom-call(s32[2,128]{1,0:T(2,128)} %get-tuple-element.9.target_ref, f32[2,128]{1,0:T(2,128)} %bitcast.44, bf16[512,1536]{1,0:T(8,128)(2,1)} %bitcast.37, bf16[128,1536]{1,0:T(8,128)(2,1)} %frames_ref.3, bf16[128,1536]{1,0:T(8,128)(2,1)} %get-tuple-element.11.grad_ref), custom_call_target="tpu_custom_call" | custom-call | flops 402653184 | bytes 2752512 | tf_op jit(solution)/shard_map/mix/pallas_call | solution.py:202
  105.8 1.3 collective-permute-start.3
  107.1 3.0 %collective-permute-start.2 = (bf16[4,1536]{1,0:T(4,128)(2,1)S(1)}, bf16[4,1536]{1,0:T(4,128)(2,1)S(1)}, u32[]{:S(2)}, u32[]{:S(2)}) collective-permute-start(bf16[4,1536]{1,0:T(4,128)(2,1)S(1)} %get-tuple-element.16), channel_id=1, source_target_pairs={{0,1},{1,2},{2,3},{3,4},{4,5},{5,6},{6,7},{7,8},{8,9},{9,10},{10,1... | collective-permute-start | bytes 36872 | tf_op jit(solution)/shard_map/ppermute | solution.py:323
  110.2 14.7 %all-to-all-done.3 = bf16[32,16,1536]{2,1,0:T(8,128)(2,1)S(1)} async-done(((bf16[32,16,1536]{2,1,0:T(8,128)(2,1)}), bf16[32,16,1536]{2,1,0:T(8,128)(2,1)S(1)}, u32[]{:S(2)}, u32[]{:S(2)}) %all-to-all-start.3) | async-done | bytes 1572896 | tf_op jit(solution)/shard_map/all_to_all | solution.py:330
  124.8 1.2 copy-done.2
  126.0 3.7 %finish.1 = bf16[128,1536]{1,0:T(8,128)(2,1)} custom-call(s32[2,128]{1,0:T(2,128)} %get-tuple-element.9.target_ref, f32[2,128]{1,0:T(2,128)} %bitcast.45, bf16[512,1536]{1,0:T(8,128)(2,1)} %bitcast.36, bf16[128,1536]{1,0:T(8,128)(2,1)} %get-tuple-element.11.grad_ref), custom_call_target="tpu_custom_call" | custom-call | flops 402653184 | bytes 2359296 | tf_op jit(solution)/shard_map/finish/pallas_call | solution.py:302
  130.3 4.2 %head.1 = bf16[527,128]{1,0:T(8,128)(2,1)} custom-call(bf16[4,1536]{1,0:T(4,128)(2,1)} %copy-done.7, bf16[128,1536]{1,0:T(8,128)(2,1)} %get-tuple-element.12.block_ref, bf16[4,1536]{1,0:T(4,128)(2,1)} %copy-done.6, f32[9,1536]{1,0:T(8,128)} %taps_ref.3, bf16[527,1536]{1,0:T(8,128)(2,1)} %bitcast.35), custom_call_target="tpu_custom_call" | custom-call | flops 207224832 | bytes 2012160 | tf_op jit(solution)/shard_map/head/pallas_call | solution.py:259
  (25 shorter events, 3.2 us)
Async XLA Ops:
  0.6 12.1 %copy-start = (bf16[128,527]{0,1:T(8,128)(2,1)S(1)}, bf16[128,527]{0,1:T(8,128)(2,1)}, u32[]{:S(2)}) copy-start(bf16[128,527]{0,1:T(8,128)(2,1)} %param.15) | copy-start | bytes 404740
  0.6 12.1 %copy-start.1 = (bf16[1536,527]{0,1:T(8,128)(2,1)S(1)}, bf16[1536,527]{0,1:T(8,128)(2,1)}, u32[]{:S(2)}) copy-start(bf16[1536,527]{0,1:T(8,128)(2,1)} %param.14) | copy-start | bytes 4856836
  4.4 32.2 %all-to-all-start = ((bf16[32,16,1536]{2,1,0:T(8,128)(2,1)}), bf16[32,16,1536]{2,1,0:T(8,128)(2,1)S(1)}, u32[]{:S(2)}, u32[]{:S(2)}) async-start(bf16[32,16,1536]{2,1,0:T(8,128)(2,1)} %bitcast.39), calls=%async_computation | async-start | bytes 3145728 | tf_op jit(solution)/shard_map/all_to_all | solution.py:330
  13.2 0.7 copy-start.5
  14.0 4.3 %collective-permute-start.1 = (bf16[4,1536]{1,0:T(4,128)(2,1)S(1)}, bf16[4,1536]{1,0:T(4,128)(2,1)S(1)}, u32[]{:S(2)}, u32[]{:S(2)}) collective-permute-start(bf16[4,1536]{1,0:T(4,128)(2,1)S(1)} %get-tuple-element.17), channel_id=1, source_target_pairs={{1,0},{2,1},{3,2},{4,3},{5,4},{6,5},{7,6},{8,7},{9,8},{10,9},{11,1... | collective-permute-start | bytes 36872 | tf_op jit(solution)/shard_map/ppermute | solution.py:324
  15.3 3.9 %collective-permute-start = (bf16[4,1536]{1,0:T(4,128)(2,1)S(1)}, bf16[4,1536]{1,0:T(4,128)(2,1)S(1)}, u32[]{:S(2)}, u32[]{:S(2)}) collective-permute-start(bf16[4,1536]{1,0:T(4,128)(2,1)S(1)} %get-tuple-element.18), channel_id=1, source_target_pairs={{0,1},{1,2},{2,3},{3,4},{4,5},{5,6},{6,7},{7,8},{8,9},{9,10},{10,1... | collective-permute-start | bytes 36872 | tf_op jit(solution)/shard_map/ppermute | solution.py:323
  18.4 0.8 copy-start.8
  19.2 0.6 copy-start.9
  36.6 31.2 %all-to-all-start.2 = ((bf16[32,16,1536]{2,1,0:T(8,128)(2,1)}), bf16[32,16,1536]{2,1,0:T(8,128)(2,1)S(1)}, u32[]{:S(2)}, u32[]{:S(2)}) async-start(bf16[32,16,1536]{2,1,0:T(8,128)(2,1)} %bitcast.41), calls=%async_computation.2 | async-start | bytes 3145728 | tf_op jit(solution)/shard_map/all_to_all | solution.py:330
  49.6 2.0 %copy-start.10 = (f32[512,2048]{1,0:T(8,128)}, f32[512,2048]{1,0:T(8,128)S(1)}, u32[]{:S(2)}) copy-start(f32[512,2048]{1,0:T(8,128)S(1)} %fusion.6) | copy-start | bytes 12582916
  67.8 1.2 copy-start.4
  69.1 27.9 %all-to-all-start.1 = ((bf16[32,16,1536]{2,1,0:T(8,128)(2,1)}), bf16[32,16,1536]{2,1,0:T(8,128)(2,1)S(1)}, u32[]{:S(2)}, u32[]{:S(2)}) async-start(bf16[32,16,1536]{2,1,0:T(8,128)(2,1)} %bitcast.6), calls=%async_computation.1 | async-start | bytes 3145728 | tf_op jit(solution)/shard_map/all_to_all | solution.py:330
  96.9 4.0 %copy-start.3 = (bf16[32,16,1536]{2,1,0:T(8,128)(2,1)}, bf16[32,16,1536]{2,1,0:T(8,128)(2,1)S(1)}, u32[]{:S(2)}) copy-start(bf16[32,16,1536]{2,1,0:T(8,128)(2,1)S(1)} %all-to-all-done.1) | copy-start | bytes 4718596
  96.9 27.9 %all-to-all-start.3 = ((bf16[32,16,1536]{2,1,0:T(8,128)(2,1)}), bf16[32,16,1536]{2,1,0:T(8,128)(2,1)S(1)}, u32[]{:S(2)}, u32[]{:S(2)}) async-start(bf16[32,16,1536]{2,1,0:T(8,128)(2,1)} %bitcast.40), calls=%async_computation.3 | async-start | bytes 3145728 | tf_op jit(solution)/shard_map/all_to_all | solution.py:330
  105.8 23.9 %collective-permute-start.3 = (bf16[4,1536]{1,0:T(4,128)(2,1)S(1)}, bf16[4,1536]{1,0:T(4,128)(2,1)S(1)}, u32[]{:S(2)}, u32[]{:S(2)}) collective-permute-start(bf16[4,1536]{1,0:T(4,128)(2,1)S(1)} %get-tuple-element.15), channel_id=1, source_target_pairs={{1,0},{2,1},{3,2},{4,3},{5,4},{6,5},{7,6},{8,7},{9,8},{10,9},{11,1... | collective-permute-start | bytes 36872 | tf_op jit(solution)/shard_map/ppermute | solution.py:324
  107.1 22.6 %collective-permute-start.2 = (bf16[4,1536]{1,0:T(4,128)(2,1)S(1)}, bf16[4,1536]{1,0:T(4,128)(2,1)S(1)}, u32[]{:S(2)}, u32[]{:S(2)}) collective-permute-start(bf16[4,1536]{1,0:T(4,128)(2,1)S(1)} %get-tuple-element.16), channel_id=1, source_target_pairs={{0,1},{1,2},{2,3},{3,4},{4,5},{5,6},{6,7},{7,8},{8,9},{9,10},{10,1... | collective-permute-start | bytes 36872 | tf_op jit(solution)/shard_map/ppermute | solution.py:323
  124.8 1.2 copy-start.2
  129.7 0.6 copy-start.6
  129.7 0.6 copy-start.7

commit v2 on v1

v2 whole, which is shorter than its diff:
```python
import functools

import jax
import jax.numpy as jnp
from jax import lax
from jax.experimental import pallas as pl
from jax.experimental.pallas import tpu as pltpu
from jax.sharding import PartitionSpec as P


slope_coef = 0.7978845608028654
cubic_coef = 0.044715
bf16 = jnp.bfloat16
f32 = jnp.float32
i32 = jnp.int32


def gelu_value(inputs):
    return (
        0.5
        * inputs
        * (1.0 + jnp.tanh(slope_coef * (inputs + cubic_coef * inputs * inputs * inputs)))
    )


def gelu_slope(inputs):
    inner = jnp.tanh(slope_coef * (inputs + cubic_coef * inputs * inputs * inputs))
    return 0.5 * (1.0 + inner) + 0.5 * inputs * (1.0 - inner * inner) * slope_coef * (
        1.0 + 3.0 * cubic_coef * inputs * inputs
    )


def cost(flops, moved):
    return pl.CostEstimate(flops=flops, bytes_accessed=moved, transcendentals=0)


def params(mib):
    return pltpu.CompilerParams(vmem_limit_bytes=mib << 20)


def resident(count):
    return [pl.BlockSpec(memory_space=pltpu.VMEM)] * count


def tiles(width, tile=512):
    return [slice(start, start + tile) for start in range(0, width, tile)]


def iota(shape, dim):
    return lax.broadcasted_iota(i32, shape, dim)


def to_column(row):
    n = row.shape[1]
    diagonal = iota((n, n), 0) == iota((n, n), 1)
    return jnp.sum(jnp.where(diagonal, row, jnp.zeros_like(row)), axis=1, keepdims=True)


def to_row(column):
    n = column.shape[0]
    diagonal = iota((n, n), 0) == iota((n, n), 1)
    return jnp.sum(jnp.where(diagonal, column, jnp.zeros_like(column)), axis=0, keepdims=True)


def send_mask(target, slots):
    rows = iota((slots, target.shape[1]), 0)
    hit = (rows == target[0:1, :]) | (rows == target[1:2, :])
    return jnp.where(hit, 1.0, 0.0).astype(bf16)


def pick_mask(target_row, slots):
    column = to_column(target_row)
    return jnp.where(iota((column.shape[0], slots), 1) == column, 1.0, 0.0).astype(bf16)


def convolve(padded, taps_ref, part, rows, first_row, step):
    taps = taps_ref.shape[0]
    summed = jnp.zeros((rows, part.stop - part.start), f32)
    for offset in range(taps):
        start = first_row + (offset if step == 1 else taps - 1 - offset)
        summed = summed + taps_ref[offset : offset + 1, part] * padded[start : start + rows, part]
    return summed


def inner_rows(block_ref, padded):
    rows, width = block_ref.shape
    padded[0:8, :] = jnp.zeros((8, width), f32)
    padded[8 : 8 + rows, :] = block_ref[...].astype(f32)
    padded[8 + rows : 16 + rows, :] = jnp.zeros((8, width), f32)


def outer_rows(low_ref, edge_ref, high_ref, padded):
    margin = low_ref.shape[0]
    padded[8 - margin : 8, :] = low_ref[...].astype(f32)
    padded[8:24, :] = edge_ref[...].astype(f32)
    padded[24 : 24 + margin, :] = high_ref[...].astype(f32)


def at_ends(low, high, rows):
    margin, n = low.shape
    gap = jnp.zeros((8 - margin, n), f32)
    middle = jnp.zeros((rows - 16, n), f32)
    return jnp.concatenate([low, gap, middle, gap, high], axis=0)


def iota(shape, dim):
    return lax.broadcasted_iota(i32, shape, dim)


def to_column(row):
    n = row.shape[1]
    diagonal = iota((n, n), 0) == iota((n, n), 1)
    return jnp.sum(jnp.where(diagonal, row, jnp.zeros_like(row)), axis=1, keepdims=True)


def to_row(column):
    n = column.shape[0]
    diagonal = iota((n, n), 0) == iota((n, n), 1)
    return jnp.sum(jnp.where(diagonal, column, jnp.zeros_like(column)), axis=0, keepdims=True)


def send_mask(target, slots):
    rows = iota((slots, target.shape[1]), 0)
    hit = (rows == target[0:1, :]) | (rows == target[1:2, :])
    return jnp.where(hit, 1.0, 0.0).astype(bf16)


def pick_mask(target_row, slots):
    column = to_column(target_row)
    return jnp.where(iota((column.shape[0], slots), 1) == column, 1.0, 0.0).astype(bf16)


def slot_targets(ids, owners, capacity):
    count = ids.shape[1]
    first, second = ids[0:1, :], ids[1:2, :]
    experts = iota((owners, count), 0)
    first_hot = jnp.where(experts == first, 1.0, 0.0)
    second_hot = jnp.where(experts == second, 1.0, 0.0)
    before = jnp.where(iota((count, count), 0) < iota((count, count), 1), 1.0, 0.0).astype(bf16)
    first_seen = jnp.dot(first_hot.astype(bf16), before, preferred_element_type=f32)
    second_seen = jnp.dot(second_hot.astype(bf16), before, preferred_element_type=f32)
    second_seen = second_seen + jnp.sum(first_hot, axis=1, keepdims=True)
    first_rank = jnp.sum(first_seen * first_hot, axis=0, keepdims=True).astype(i32)
    second_rank = jnp.sum(second_seen * second_hot, axis=0, keepdims=True).astype(i32)
    return jnp.concatenate(
        [first * capacity + first_rank, second * capacity + second_rank], axis=0
    )


def dispatch_kernel(owners, capacity, ids_ref, frames_ref, send_ref, target_ref):
    target = slot_targets(ids_ref[...], owners, capacity)
    target_ref[...] = target
    mask = send_mask(target, owners * capacity)
    for part in tiles(frames_ref.shape[1]):
        send_ref[:, part] = jnp.dot(
            mask, frames_ref[:, part], preferred_element_type=f32
        ).astype(bf16)


def dispatch(ids, frames, owners, capacity):
    rows, width = frames.shape
    slots = owners * capacity
    return pl.pallas_call(
        functools.partial(dispatch_kernel, owners, capacity),
        out_shape=(
            jax.ShapeDtypeStruct((slots, width), bf16),
            jax.ShapeDtypeStruct((2, rows), i32),
        ),
        in_specs=resident(2),
        out_specs=tuple(resident(2)),
        cost_estimate=cost(2 * slots * rows * width, 2 * (slots + rows) * width),
        compiler_params=params(60),
        name="dispatch",
    )(ids, frames)


def keep_edges(block_ref, edge_ref):
    rows = block_ref.shape[0]
    edge_ref[0:8, :] = block_ref[0:8, :]
    edge_ref[8:16, :] = block_ref[rows - 8 : rows, :]


def grad_inner_kernel(block_ref, taps_ref, inner_ref, edge_ref, padded):
    rows, width = block_ref.shape
    inner_rows(block_ref, padded)
    keep_edges(block_ref, edge_ref)
    start = 8 - taps_ref.shape[0] // 2
    for part in tiles(width):
        inner_ref[:, part] = convolve(padded, taps_ref, part, rows, start, -1).astype(bf16)


def grad_inner(block, taps):
    rows, width = block.shape
    return pl.pallas_call(
        grad_inner_kernel,
        out_shape=(
            jax.ShapeDtypeStruct((rows, width), bf16),
            jax.ShapeDtypeStruct((16, width), bf16),
        ),
        in_specs=resident(2),
        out_specs=tuple(resident(2)),
        scratch_shapes=[pltpu.VMEM((rows + 16, width), f32)],
        cost_estimate=cost(18 * rows * width, 4 * rows * width),
        compiler_params=params(8),
        name="grad_inner",
    )(block, taps)


def grad_kernel(
    target_ref, low_ref, edge_ref, high_ref, inner_ref, taps_ref, grad_ref, send_ref, padded
):
    rows, width = inner_ref.shape
    margin = low_ref.shape[0]
    outer_rows(low_ref, edge_ref, high_ref, padded)
    mask = send_mask(target_ref[...], send_ref.shape[0])
    frame = iota((rows, 1), 0)
    outer = (frame < margin) | (frame >= rows - margin)
    for part in tiles(width):
        first = convolve(padded, taps_ref, part, margin, 8 - margin, -1)
        last = convolve(padded, taps_ref, part, margin, 24 - 2 * margin, -1)
        ends = at_ends(first, last, rows)
        grad = jnp.where(outer, ends, inner_ref[:, part].astype(f32)).astype(bf16)
        grad_ref[:, part] = grad
        send_ref[:, part] = jnp.dot(mask, grad, preferred_element_type=f32).astype(bf16)


def grad_dispatch(target, low, edge, high, inner, taps, slots):
    rows, width = inner.shape
    return pl.pallas_call(
        grad_kernel,
        out_shape=(
            jax.ShapeDtypeStruct((rows, width), bf16),
            jax.ShapeDtypeStruct((slots, width), bf16),
        ),
        in_specs=resident(6),
        out_specs=tuple(resident(2)),
        scratch_shapes=[pltpu.VMEM((32, width), f32)],
        cost_estimate=cost(2 * slots * rows * width, 2 * (slots + 2 * rows) * width),
        compiler_params=params(8),
        name="grad_dispatch",
    )(target, low, edge, high, inner, taps)


def mix_kernel(target_ref, gates_ref, slots_ref, frames_ref, grad_ref, mixed_ref, gate_grad_ref):
    rows, width = frames_ref.shape
    slots = slots_ref.shape[0]
    masks = [pick_mask(target_ref[k : k + 1, :], slots) for k in range(2)]
    gates = [to_column(gates_ref[k : k + 1, :]) for k in range(2)]
    sums = [jnp.zeros((rows, 1), f32) for _ in range(2)]
    for part in tiles(width):
        grad = grad_ref[:, part].astype(f32)
        mixed = frames_ref[:, part].astype(f32)
        for k in range(2):
            picked = jnp.dot(masks[k], slots_ref[:, part], preferred_element_type=f32)
            mixed = mixed + gates[k] * picked
            sums[k] = sums[k] + jnp.sum(picked * grad, axis=1, keepdims=True)
        mixed_ref[:, part] = mixed.astype(bf16)
    for k in range(2):
        gate_grad_ref[k : k + 1, :] = to_row(sums[k])


def mix(target, gates, slots, frames, grad):
    rows, width = frames.shape
    n = slots.shape[0]
    return pl.pallas_call(
        mix_kernel,
        out_shape=(
            jax.ShapeDtypeStruct((rows, width), bf16),
            jax.ShapeDtypeStruct((2, rows), f32),
        ),
        in_specs=resident(5),
        out_specs=tuple(resident(2)),
        cost_estimate=cost(4 * n * rows * width, 2 * (n + 3 * rows) * width),
        compiler_params=params(60),
        name="mix",
    )(target, gates, slots, frames, grad)


def classes_of(head_ref, part, smooth):
    return lax.dot_general(
        head_ref[:, part], smooth, (((1,), (1,)), ((), ())), preferred_element_type=f32
    )


def head_inner_kernel(block_ref, taps_ref, head_ref, logits_ref, edge_ref, padded):
    rows, width = block_ref.shape
    inner_rows(block_ref, padded)
    keep_edges(block_ref, edge_ref)
    total = jnp.zeros(logits_ref.shape, f32)
    start = 8 - taps_ref.shape[0] // 2
    for part in tiles(width):
        smooth = convolve(padded, taps_ref, part, rows, start, 1).astype(bf16)
        total = total + classes_of(head_ref, part, smooth)
    logits_ref[...] = total.astype(bf16)


def head_inner(block, taps, head_t):
    rows, width = block.shape
    classes = head_t.shape[0]
    return pl.pallas_call(
        head_inner_kernel,
        out_shape=(
            jax.ShapeDtypeStruct((classes, rows), bf16),
            jax.ShapeDtypeStruct((16, width), bf16),
        ),
        in_specs=resident(3),
        out_specs=tuple(resident(2)),
        scratch_shapes=[pltpu.VMEM((rows + 16, width), f32)],
        cost_estimate=cost(2 * classes * rows * width, 2 * (classes + rows) * width),
        compiler_params=params(8),
        name="head_inner",
    )(block, taps, head_t)


def head_outer_kernel(
    low_ref, edge_ref, high_ref, taps_ref, head_ref, inner_ref, logits_ref, padded
):
    rows = inner_ref.shape[1]
    width = edge_ref.shape[1]
    margin = low_ref.shape[0]
    outer_rows(low_ref, edge_ref, high_ref, padded)
    total = jnp.zeros(inner_ref.shape, f32)
    for part in tiles(width):
        first = convolve(padded, taps_ref, part, margin, 8 - margin, 1)
        last = convolve(padded, taps_ref, part, margin, 24 - 2 * margin, 1)
        total = total + classes_of(head_ref, part, at_ends(first, last, rows).astype(bf16))
    frame = iota((1, rows), 1)
    outer = (frame < margin) | (frame >= rows - margin)
    logits_ref[...] = jnp.where(outer, total, inner_ref[...].astype(f32)).astype(bf16)


def head_outer(low, edge, high, taps, head_t, inner):
    classes, rows = inner.shape
    width = edge.shape[1]
    return pl.pallas_call(
        head_outer_kernel,
        out_shape=jax.ShapeDtypeStruct((classes, rows), bf16),
        in_specs=resident(6),
        out_specs=resident(1)[0],
        scratch_shapes=[pltpu.VMEM((32, width), f32)],
        cost_estimate=cost(2 * classes * rows * width, 2 * (classes + rows) * width),
        compiler_params=params(8),
        name="head_outer",
    )(low, edge, high, taps, head_t, inner)


def finish_kernel(target_ref, gates_ref, slots_ref, grad_ref, out_ref):
    slots = slots_ref.shape[0]
    masks = [pick_mask(target_ref[k : k + 1, :], slots) for k in range(2)]
    gates = [to_column(gates_ref[k : k + 1, :]) for k in range(2)]
    for part in tiles(grad_ref.shape[1]):
        total = grad_ref[:, part].astype(f32)
        for k in range(2):
            total = total + gates[k] * jnp.dot(
                masks[k], slots_ref[:, part], preferred_element_type=f32
            )
        out_ref[:, part] = total.astype(bf16)


def finish(target, gates, slots, grad):
    rows, width = grad.shape
    n = slots.shape[0]
    return pl.pallas_call(
        finish_kernel,
        out_shape=jax.ShapeDtypeStruct((rows, width), bf16),
        in_specs=resident(4),
        out_specs=resident(1)[0],
        cost_estimate=cost(4 * n * rows * width, 2 * (n + 2 * rows) * width),
        compiler_params=params(8),
        name="finish",
    )(target, gates, slots, grad)


def keep_kernel(gates_ref, out_ref):
    out_ref[...] = gates_ref[...]


def keep(gates):
    return pl.pallas_call(
        keep_kernel,
        out_shape=jax.ShapeDtypeStruct(gates.shape, gates.dtype),
        in_specs=resident(1),
        out_specs=resident(1)[0],
        compiler_params=pltpu.CompilerParams(vmem_limit_bytes=67043328 - 1000000),
        name="keep",
    )(gates)


def edges(block, width):
    axes = ("seq", "expert")
    count = lax.axis_size(axes)
    forward = [(i, i + 1) for i in range(count - 1)]
    backward = [(target, source) for source, target in forward]
    low = lax.ppermute(block[block.shape[0] - width :], axes, forward)
    high = lax.ppermute(block[:width], axes, backward)
    return low, high


def exchange(slots, owners):
    blocks = slots.reshape(owners, -1, slots.shape[1])
    blocks = lax.all_to_all(blocks, "expert", split_axis=0, concat_axis=0, tiled=True)
    return blocks.reshape(slots.shape)


def layer(
    frames, expert_ids, gate_weights, up_weight, down_weight, smooth_taps, head_weight, logit_grad
):
    owners = lax.axis_size("expert")
    local_rows = frames.shape[0]
    capacity = 4 * local_rows // owners
    slots = owners * capacity
    margin = smooth_taps.shape[0] // 2
    up_one = up_weight[0]
    down_one = down_weight[0]
    gates = gate_weights.T
    head_t = head_weight.T

    send_x, target = dispatch(expert_ids.T, frames, owners, capacity)
    got_x = exchange(send_x, owners)

    smooth_grad = jnp.einsum(
        "fc,dc->fd", logit_grad, head_weight, preferred_element_type=f32
    ).astype(bf16)
    smooth_grad = lax.optimization_barrier(smooth_grad)
    low, high = edges(smooth_grad, margin)
    inner_grad, edge = grad_inner(smooth_grad, smooth_taps)
    mixed_grad, send_g = grad_dispatch(target, low, edge, high, inner_grad, smooth_taps, slots)
    got_g = exchange(send_g, owners)

    pre = jnp.dot(got_x, up_one, preferred_element_type=f32)
    hidden = gelu_value(pre).astype(bf16)
    outputs = jnp.dot(hidden, down_one, preferred_element_type=f32).astype(bf16)
    out_slots = exchange(outputs, owners)
    mix_gates = keep(gates)

    back_hidden = jnp.einsum("rd,hd->rh", got_g, down_one, preferred_element_type=f32)
    pre_grad = (back_hidden * gelu_slope(pre)).astype(bf16)
    parts = jnp.einsum("rh,dh->rd", pre_grad, up_one, preferred_element_type=f32).astype(bf16)
    part_slots = exchange(parts, owners)

    mixed, gate_grad = mix(target, mix_gates, out_slots, frames, mixed_grad)
    low, high = edges(mixed, margin)
    inner_logits, edge = head_inner(mixed, smooth_taps, head_t)
    logits = head_outer(low, edge, high, smooth_taps, head_t, inner_logits)
    frame_grad = finish(target, gates, part_slots, mixed_grad)
    return (logits.T, frame_grad, gate_grad.T)


def solution(mesh):
    placed = (
        P(("seq", "expert"), None),
        P(("seq", "expert"), None),
        P(("seq", "expert"), None),
        P("expert", None, None),
        P("expert", None, None),
        P(),
        P(),
        P(("seq", "expert"), None),
    )
    return jax.shard_map(
        layer,
        mesh=mesh,
        in_specs=placed,
        out_specs=(
            P(("seq", "expert"), None),
            P(("seq", "expert"), None),
            P(("seq", "expert"), None),
        ),
        check_vma=False,
    )
```

time: 135 us -> 127 us (0.941)
  Pallas kernels: 20 us -> 16.2 us
  waiting for transfers between devices: 46.1 us -> 43.2 us
    pallas_call x5 -> x8, Pallas kernels: 20 us -> 16.2 us  [the longest x1 3.21 us: mix(): pl.pallas_call(mix_kernel, out_shape=(jax.ShapeDtypeStruct((rows, width),...]
    all_to_all x4, waiting for transfers between devices: 45.3 us -> 43.2 us  [exchange(): lax.all_to_all(blocks, 'expert', split_axis=0, concat_axis=0, tiled=True)]
    unnamed x22 -> x24, local copies, waits for them, and re-layouts: 6.28 us -> 5.15 us
  transfers between devices with their start and end apart: 8 -> 8, of which waited for: 5 -> 4; matrix products, arithmetic and copies ran while one was open for 22% -> 23% of each run, Pallas kernels for 9% -> 9%
where the time goes in v2:
time: 127 us; the launch traced here: 126 us
  waiting for transfers between devices  43.2 us (34%)
  starting transfers between devices  31.7 us (25%)
  matrix products  28.5 us (22%)
  Pallas kernels  16.2 us (13%)
  local copies, waits for them, and re-layouts  5.93 us (5%)
    all_to_all x4, waiting for transfers between devices, exchange(): lax.all_to_all(blocks, 'expert', split_axis=0, concat_axis=0, tiled=True)  43.2 us
    all_to_all x4, starting transfers between devices, exchange(): lax.all_to_all(blocks, 'expert', split_axis=0, concat_axis=0, tiled=True)  23.1 us
    dot_general x1, matrix products, layer(): jnp.einsum('rh,dh->rd', pre_grad, up_one, preferred_element_type=f32)  14.3 us
    dot_general x1, matrix products, layer(): outputs = jnp.dot(hidden, down_one, preferred_element_type=f32).astype(bf16)  7.72 us
    ppermute x2, starting transfers between devices, edges(): low = lax.ppermute(block[block.shape[0] - width:], axes, forward)  6.06 us
    dot_general x1, matrix products, layer(): pre = jnp.dot(got_x, up_one, preferred_element_type=f32)  5.99 us
    unnamed x24, local copies, waits for them, and re-layouts  5.15 us
    pallas_call x1, Pallas kernels, mix(): pl.pallas_call(mix_kernel, out_shape=(jax.ShapeDtypeStruct((rows, width),...  3.21 us
  transfers between devices with their start and end apart: 8, of which 4 were waited for; matrix products, arithmetic and copies ran while one was open for 23% of the time, Pallas kernels for 9%

profile of v2, /device:TPU:0, one launch (start us, length us, event | category | flops | bytes accessed | tf_op | source)
XLA Modules:
  0.0 126.3 jit_solution(2839163884964768453)
XLA Ops:
  0.7 3.0 %dispatch.1 = (bf16[512,1536]{1,0:T(8,128)(2,1)}, s32[2,128]{1,0:T(2,128)}) custom-call(s32[2,128]{1,0:T(2,128)} %bitcast.42, bf16[128,1536]{1,0:T(8,128)(2,1)} %frames_ref.3), custom_call_target="tpu_custom_call" | custom-call | flops 201326592 | bytes 1966080 | tf_op jit(solution)/shard_map/dispatch/pallas_call | solution.py:163
  3.7 8.5 %all-to-all-start = ((bf16[32,16,1536]{2,1,0:T(8,128)(2,1)}), bf16[32,16,1536]{2,1,0:T(8,128)(2,1)}, u32[]{:S(2)}, u32[]{:S(2)}) async-start(bf16[32,16,1536]{2,1,0:T(8,128)(2,1)} %bitcast.39), calls=%async_computation | async-start | bytes 3145728 | tf_op jit(solution)/shard_map/all_to_all | solution.py:401
  12.7 1.3 %collective-permute-start.1 = (bf16[4,1536]{1,0:T(4,128)(2,1)S(1)}, bf16[4,1536]{1,0:T(4,128)(2,1)S(1)}, u32[]{:S(2)}, u32[]{:S(2)}) collective-permute-start(bf16[4,1536]{1,0:T(4,128)(2,1)S(1)} %get-tuple-element.25), channel_id=1, source_target_pairs={{1,0},{2,1},{3,2},{4,3},{5,4},{6,5},{7,6},{8,7},{9,8},{10,9},{11,1... | collective-permute-start | bytes 36872 | tf_op jit(solution)/shard_map/ppermute | solution.py:395
  14.0 3.0 %collective-permute-start = (bf16[4,1536]{1,0:T(4,128)(2,1)S(1)}, bf16[4,1536]{1,0:T(4,128)(2,1)S(1)}, u32[]{:S(2)}, u32[]{:S(2)}) collective-permute-start(bf16[4,1536]{1,0:T(4,128)(2,1)S(1)} %get-tuple-element.26), channel_id=1, source_target_pairs={{0,1},{1,2},{2,3},{3,4},{4,5},{5,6},{6,7},{7,8},{8,9},{9,10},{10,1... | collective-permute-start | bytes 36872 | tf_op jit(solution)/shard_map/ppermute | solution.py:394
  17.1 1.4 %grad_inner.1 = (bf16[128,1536]{1,0:T(8,128)(2,1)S(1)}, bf16[16,1536]{1,0:T(8,128)(2,1)S(1)}) custom-call(bf16[128,1536]{1,0:T(8,128)(2,1)S(1)} %convolution_convert_fusion.block_ref, f32[9,1536]{1,0:T(8,128)S(1)} %copy-done.6), custom_call_target="tpu_custom_call" | custom-call | flops 3538944 | bytes 786432 | tf_op jit(solution)/shard_map/grad_inner/pallas_call | solution.py:194
  18.5 1.8 %grad_dispatch.1 = (bf16[128,1536]{1,0:T(8,128)(2,1)S(1)}, bf16[512,1536]{1,0:T(8,128)(2,1)}) custom-call(s32[2,128]{1,0:T(2,128)S(1)} %copy-done.8, bf16[4,1536]{1,0:T(4,128)(2,1)S(1)} %collective-permute-done.low_ref, bf16[16,1536]{1,0:T(8,128)(2,1)S(1)} %get-tuple-element.15.edge_ref, bf16[4,1536]{1,0:T(4,128)(2,1)S(1)} %collective-permute-done.1.high_ref, ...), custom_call_target="tpu_custom_call" | custom-call | flops 201326592 | bytes 2359296 | tf_op jit(solution)/shard_map/grad_dispatch/pallas_call | solution.py:229
  21.0 15.0 %all-to-all-done = bf16[32,16,1536]{2,1,0:T(8,128)(2,1)} async-done(((bf16[32,16,1536]{2,1,0:T(8,128)(2,1)}), bf16[32,16,1536]{2,1,0:T(8,128)(2,1)}, u32[]{:S(2)}, u32[]{:S(2)}) %all-to-all-start) | async-done | bytes 1572896 | tf_op jit(solution)/shard_map/all_to_all | solution.py:401
  36.1 5.0 %all-to-all-start.2 = ((bf16[32,16,1536]{2,1,0:T(8,128)(2,1)}), bf16[32,16,1536]{2,1,0:T(8,128)(2,1)S(1)}, u32[]{:S(2)}, u32[]{:S(2)}) async-start(bf16[32,16,1536]{2,1,0:T(8,128)(2,1)} %bitcast.10), calls=%async_computation.2 | async-start | bytes 3145728 | tf_op jit(solution)/shard_map/all_to_all | solution.py:401
  41.1 6.0 %fusion.6 = f32[512,2048]{1,0:T(8,128)S(1)} fusion(bf16[512,1536]{1,0:T(8,128)(2,1)} %bitcast.3, bf16[1,1536,2048]{2,1,0:T(8,128)(2,1)} %param.11), kind=kOutput, calls=%fused_computation.6 | convolution fusion | flops 3221225472 | bytes 12058624 | tf_op jit(solution)/shard_map/dot_general | solution.py:430
  47.1 1.9 %copy-done.11 = f32[512,2048]{1,0:T(8,128)} copy-done((f32[512,2048]{1,0:T(8,128)}, f32[512,2048]{1,0:T(8,128)S(1)}, u32[]{:S(2)}) %copy-start.11) | copy-done | bytes 4194328
  49.0 7.7 %fusion.20 = bf16[512,1536]{1,0:T(8,128)(2,1)} fusion(bf16[1,2048,1536]{2,1,0:T(8,128)(2,1)} %param.12, f32[512,2048]{1,0:T(8,128)S(1)} %fusion.6), kind=kOutput, calls=%fused_computation.19 | convolution fusion | flops 3231449088 | bytes 12058624 | tf_op jit(solution)/shard_map/dot_general | solution.py:432
  56.7 8.2 %all-to-all-done.2 = bf16[32,16,1536]{2,1,0:T(8,128)(2,1)S(1)} async-done(((bf16[32,16,1536]{2,1,0:T(8,128)(2,1)}), bf16[32,16,1536]{2,1,0:T(8,128)(2,1)S(1)}, u32[]{:S(2)}, u32[]{:S(2)}) %all-to-all-start.2) | async-done | bytes 1572896 | tf_op jit(solution)/shard_map/all_to_all | solution.py:401
  65.0 4.9 %all-to-all-start.1 = ((bf16[32,16,1536]{2,1,0:T(8,128)(2,1)}), bf16[32,16,1536]{2,1,0:T(8,128)(2,1)}, u32[]{:S(2)}, u32[]{:S(2)}) async-start(bf16[32,16,1536]{2,1,0:T(8,128)(2,1)} %bitcast.6), calls=%async_computation.1 | async-start | bytes 3145728 | tf_op jit(solution)/shard_map/all_to_all | solution.py:401
  69.8 14.3 %fusion.17 = bf16[512,1536]{1,0:T(8,128)(2,1)} fusion(bf16[1,1536,2048]{2,1,0:T(8,128)(2,1)} %param.11, f32[512,2048]{1,0:T(8,128)} %copy-done.11, bf16[512,1536]{1,0:T(8,128)(2,1)S(1)} %bitcast.40, bf16[1,2048,1536]{2,1,0:T(8,128)(2,1)} %param.12), kind=kOutput, calls=%fused_computation.18 | convolution fusion | flops 6463160320 | bytes 19922944 | tf_op jit(solution)/shard_map/rh,dh->rd/dot_general | solution.py:438
  84.2 9.4 %all-to-all-done.1 = bf16[32,16,1536]{2,1,0:T(8,128)(2,1)} async-done(((bf16[32,16,1536]{2,1,0:T(8,128)(2,1)}), bf16[32,16,1536]{2,1,0:T(8,128)(2,1)}, u32[]{:S(2)}, u32[]{:S(2)}) %all-to-all-start.1) | async-done | bytes 1572896 | tf_op jit(solution)/shard_map/all_to_all | solution.py:401
  93.6 4.7 %all-to-all-start.3 = ((bf16[32,16,1536]{2,1,0:T(8,128)(2,1)}), bf16[32,16,1536]{2,1,0:T(8,128)(2,1)}, u32[]{:S(2)}, u32[]{:S(2)}) async-start(bf16[32,16,1536]{2,1,0:T(8,128)(2,1)} %bitcast.12), calls=%async_computation.3 | async-start | bytes 3145728 | tf_op jit(solution)/shard_map/all_to_all | solution.py:401
  99.5 3.2 %mix.1 = (bf16[128,1536]{1,0:T(8,128)(2,1)}, f32[2,128]{1,0:T(2,128)}) custom-call(s32[2,128]{1,0:T(2,128)} %get-tuple-element.13.target_ref, f32[2,128]{1,0:T(2,128)} %keep.1.gates_ref, bf16[512,1536]{1,0:T(8,128)(2,1)} %bitcast.7.slots_ref, bf16[128,1536]{1,0:T(8,128)(2,1)} %frames_ref.3, bf16[128,1536]{1,0:T(8,128)(2,1)} %copy-done.4), custom_call_target="tpu_custom_call" | custom-call | flops 402653184 | bytes 2752512 | tf_op jit(solution)/shard_map/mix/pallas_call | solution.py:265
  103.5 1.3 %collective-permute-start.3 = (bf16[4,1536]{1,0:T(4,128)(2,1)S(1)}, bf16[4,1536]{1,0:T(4,128)(2,1)S(1)}, u32[]{:S(2)}, u32[]{:S(2)}) collective-permute-start(bf16[4,1536]{1,0:T(4,128)(2,1)S(1)} %get-tuple-element.23), channel_id=1, source_target_pairs={{1,0},{2,1},{3,2},{4,3},{5,4},{6,5},{7,6},{8,7},{9,8},{10,9},{11,1... | collective-permute-start | bytes 36872 | tf_op jit(solution)/shard_map/ppermute | solution.py:395
  104.8 3.0 %collective-permute-start.2 = (bf16[4,1536]{1,0:T(4,128)(2,1)S(1)}, bf16[4,1536]{1,0:T(4,128)(2,1)S(1)}, u32[]{:S(2)}, u32[]{:S(2)}) collective-permute-start(bf16[4,1536]{1,0:T(4,128)(2,1)S(1)} %get-tuple-element.24), channel_id=1, source_target_pairs={{0,1},{1,2},{2,3},{3,4},{4,5},{5,6},{6,7},{7,8},{8,9},{9,10},{10,1... | collective-permute-start | bytes 36872 | tf_op jit(solution)/shard_map/ppermute | solution.py:394
  107.8 1.4 %copy-done.2 = bf16[1536,527]{0,1:T(8,128)(2,1)S(1)} copy-done((bf16[1536,527]{0,1:T(8,128)(2,1)S(1)}, bf16[1536,527]{0,1:T(8,128)(2,1)}, u32[]{:S(2)}) %copy-start.2) | copy-done | bytes 1618968
  110.3 1.4 %head_inner.1 = (bf16[527,128]{1,0:T(8,128)(2,1)S(1)}, bf16[16,1536]{1,0:T(8,128)(2,1)S(1)}) custom-call(bf16[128,1536]{1,0:T(8,128)(2,1)S(1)} %copy-done.7, f32[9,1536]{1,0:T(8,128)S(1)} %copy-done.6, bf16[527,1536]{1,0:T(8,128)(2,1)S(1)} %bitcast.35), custom_call_target="tpu_custom_call" | custom-call | flops 207224832 | bytes 2012160 | tf_op jit(solution)/shard_map/head_inner/pallas_call | solution.py:300
  111.7 10.5 %all-to-all-done.3 = bf16[32,16,1536]{2,1,0:T(8,128)(2,1)} async-done(((bf16[32,16,1536]{2,1,0:T(8,128)(2,1)}), bf16[32,16,1536]{2,1,0:T(8,128)(2,1)}, u32[]{:S(2)}, u32[]{:S(2)}) %all-to-all-start.3) | async-done | bytes 1572896 | tf_op jit(solution)/shard_map/all_to_all | solution.py:401
  122.2 2.8 %finish.1 = bf16[128,1536]{1,0:T(8,128)(2,1)} custom-call(s32[2,128]{1,0:T(2,128)S(1)} %copy-done.9, f32[2,128]{1,0:T(2,128)S(1)} %bitcast.38, bf16[512,1536]{1,0:T(8,128)(2,1)} %bitcast.13.slots_ref, bf16[128,1536]{1,0:T(8,128)(2,1)S(1)} %copy-done.5), custom_call_target="tpu_custom_call" | custom-call | flops 402653184 | bytes 2359296 | tf_op jit(solution)/shard_map/finish/pallas_call | solution.py:363
  125.0 1.3 %head_outer.1 = bf16[527,128]{1,0:T(8,128)(2,1)} custom-call(bf16[4,1536]{1,0:T(4,128)(2,1)S(1)} %collective-permute-done.2.low_ref, bf16[16,1536]{1,0:T(8,128)(2,1)S(1)} %get-tuple-element.19.edge_ref, bf16[4,1536]{1,0:T(4,128)(2,1)S(1)} %collective-permute-done.3.high_ref, f32[9,1536]{1,0:T(8,128)S(1)} %copy-done.6, bf16[527,1536]{1,0:T(8,128)(2,1)S(1)} %bitcast.36, ...), custom_call_target="tpu_custom_call" | custom-call | flops 207224832 | bytes 2012160 | tf_op jit(solution)/shard_map/head_outer/pallas_call | solution.py:335
  (30 shorter events, 4.3 us)
Async XLA Ops:
  0.6 11.6 %copy-start = (bf16[128,527]{0,1:T(8,128)(2,1)S(1)}, bf16[128,527]{0,1:T(8,128)(2,1)}, u32[]{:S(2)}) copy-start(bf16[128,527]{0,1:T(8,128)(2,1)} %param.15) | copy-start | bytes 404740
  0.6 11.5 %copy-start.1 = (bf16[1536,527]{0,1:T(8,128)(2,1)S(1)}, bf16[1536,527]{0,1:T(8,128)(2,1)}, u32[]{:S(2)}) copy-start(bf16[1536,527]{0,1:T(8,128)(2,1)} %param.14) | copy-start | bytes 4856836
  0.7 16.4 %copy-start.6 = (f32[9,1536]{1,0:T(8,128)S(1)}, f32[9,1536]{1,0:T(8,128)}, u32[]{:S(2)}) copy-start(f32[9,1536]{1,0:T(8,128)} %taps_ref.7) | copy-start | bytes 165892
  3.7 14.8 %copy-start.8 = (s32[2,128]{1,0:T(2,128)S(1)}, s32[2,128]{1,0:T(2,128)}, u32[]{:S(2)}) copy-start(s32[2,128]{1,0:T(2,128)} %get-tuple-element.13.target_ref) | copy-start | bytes 3076
  3.7 32.4 %all-to-all-start = ((bf16[32,16,1536]{2,1,0:T(8,128)(2,1)}), bf16[32,16,1536]{2,1,0:T(8,128)(2,1)}, u32[]{:S(2)}, u32[]{:S(2)}) async-start(bf16[32,16,1536]{2,1,0:T(8,128)(2,1)} %bitcast.39), calls=%async_computation | async-start | bytes 3145728 | tf_op jit(solution)/shard_map/all_to_all | solution.py:401
  12.7 5.7 %collective-permute-start.1 = (bf16[4,1536]{1,0:T(4,128)(2,1)S(1)}, bf16[4,1536]{1,0:T(4,128)(2,1)S(1)}, u32[]{:S(2)}, u32[]{:S(2)}) collective-permute-start(bf16[4,1536]{1,0:T(4,128)(2,1)S(1)} %get-tuple-element.25), channel_id=1, source_target_pairs={{1,0},{2,1},{3,2},{4,3},{5,4},{6,5},{7,6},{8,7},{9,8},{10,9},{11,1... | collective-permute-start | bytes 36872 | tf_op jit(solution)/shard_map/ppermute | solution.py:395
  14.0 4.4 %collective-permute-start = (bf16[4,1536]{1,0:T(4,128)(2,1)S(1)}, bf16[4,1536]{1,0:T(4,128)(2,1)S(1)}, u32[]{:S(2)}, u32[]{:S(2)}) collective-permute-start(bf16[4,1536]{1,0:T(4,128)(2,1)S(1)} %get-tuple-element.26), channel_id=1, source_target_pairs={{0,1},{1,2},{2,3},{3,4},{4,5},{5,6},{6,7},{7,8},{8,9},{9,10},{10,1... | collective-permute-start | bytes 36872 | tf_op jit(solution)/shard_map/ppermute | solution.py:394
  20.3 0.7 copy-start.4
  36.1 28.9 %all-to-all-start.2 = ((bf16[32,16,1536]{2,1,0:T(8,128)(2,1)}), bf16[32,16,1536]{2,1,0:T(8,128)(2,1)S(1)}, u32[]{:S(2)}, u32[]{:S(2)}) async-start(bf16[32,16,1536]{2,1,0:T(8,128)(2,1)} %bitcast.10), calls=%async_computation.2 | async-start | bytes 3145728 | tf_op jit(solution)/shard_map/all_to_all | solution.py:401
  47.0 2.0 %copy-start.11 = (f32[512,2048]{1,0:T(8,128)}, f32[512,2048]{1,0:T(8,128)S(1)}, u32[]{:S(2)}) copy-start(f32[512,2048]{1,0:T(8,128)S(1)} %fusion.6) | copy-start | bytes 12582916
  65.0 28.6 %all-to-all-start.1 = ((bf16[32,16,1536]{2,1,0:T(8,128)(2,1)}), bf16[32,16,1536]{2,1,0:T(8,128)(2,1)}, u32[]{:S(2)}, u32[]{:S(2)}) async-start(bf16[32,16,1536]{2,1,0:T(8,128)(2,1)} %bitcast.6), calls=%async_computation.1 | async-start | bytes 3145728 | tf_op jit(solution)/shard_map/all_to_all | solution.py:401
  84.2 38.0 %copy-start.5 = (bf16[128,1536]{1,0:T(8,128)(2,1)S(1)}, bf16[128,1536]{1,0:T(8,128)(2,1)}, u32[]{:S(2)}) copy-start(bf16[128,1536]{1,0:T(8,128)(2,1)} %copy-done.4) | copy-start | bytes 1179652
  84.2 38.0 %copy-start.9 = (s32[2,128]{1,0:T(2,128)S(1)}, s32[2,128]{1,0:T(2,128)}, u32[]{:S(2)}) copy-start(s32[2,128]{1,0:T(2,128)} %get-tuple-element.13.target_ref) | copy-start | bytes 3076
  84.2 38.0 %copy-start.10 = (f32[128,2]{0,1:T(2,128)S(1)}, f32[128,2]{0,1:T(2,128)}, u32[]{:S(2)}) copy-start(f32[128,2]{0,1:T(2,128)} %param.10) | copy-start | bytes 3076
  93.6 28.6 %all-to-all-start.3 = ((bf16[32,16,1536]{2,1,0:T(8,128)(2,1)}), bf16[32,16,1536]{2,1,0:T(8,128)(2,1)}, u32[]{:S(2)}, u32[]{:S(2)}) async-start(bf16[32,16,1536]{2,1,0:T(8,128)(2,1)} %bitcast.12), calls=%async_computation.3 | async-start | bytes 3145728 | tf_op jit(solution)/shard_map/all_to_all | solution.py:401
  99.5 25.5 %copy-start.3 = (bf16[1536,527]{0,1:T(8,128)(2,1)S(1)}, bf16[1536,527]{0,1:T(8,128)(2,1)}, u32[]{:S(2)}) copy-start(bf16[1536,527]{0,1:T(8,128)(2,1)} %param.14) | copy-start | bytes 4856836
  103.5 21.5 %collective-permute-start.3 = (bf16[4,1536]{1,0:T(4,128)(2,1)S(1)}, bf16[4,1536]{1,0:T(4,128)(2,1)S(1)}, u32[]{:S(2)}, u32[]{:S(2)}) collective-permute-start(bf16[4,1536]{1,0:T(4,128)(2,1)S(1)} %get-tuple-element.23), channel_id=1, source_target_pairs={{1,0},{2,1},{3,2},{4,3},{5,4},{6,5},{7,6},{8,7},{9,8},{10,9},{11,1... | collective-permute-start | bytes 36872 | tf_op jit(solution)/shard_map/ppermute | solution.py:395
  104.8 20.2 %collective-permute-start.2 = (bf16[4,1536]{1,0:T(4,128)(2,1)S(1)}, bf16[4,1536]{1,0:T(4,128)(2,1)S(1)}, u32[]{:S(2)}, u32[]{:S(2)}) collective-permute-start(bf16[4,1536]{1,0:T(4,128)(2,1)S(1)} %get-tuple-element.24), channel_id=1, source_target_pairs={{0,1},{1,2},{2,3},{3,4},{4,5},{5,6},{6,7},{7,8},{8,9},{9,10},{10,1... | collective-permute-start | bytes 36872 | tf_op jit(solution)/shard_map/ppermute | solution.py:394
  107.8 1.4 %copy-start.2 = (bf16[1536,527]{0,1:T(8,128)(2,1)S(1)}, bf16[1536,527]{0,1:T(8,128)(2,1)}, u32[]{:S(2)}) copy-start(bf16[1536,527]{0,1:T(8,128)(2,1)} %param.14) | copy-start | bytes 4856836
  109.3 1.0 copy-start.7

commit v3 on v2

--- a/solution.py
+++ b/solution.py
@@ -42,7 +42,7 @@
     return [pl.BlockSpec(memory_space=pltpu.VMEM)] * count
 
 
-def tiles(width, tile=512):
+def tiles(width, tile=256):
     return [slice(start, start + tile) for start in range(0, width, tile)]
 
 
@@ -271,7 +271,7 @@
         in_specs=resident(5),
         out_specs=tuple(resident(2)),
         cost_estimate=cost(4 * n * rows * width, 2 * (n + 3 * rows) * width),
-        compiler_params=params(60),
+        compiler_params=params(8),
         name="mix",
     )(target, gates, slots, frames, grad)
 
@@ -282,8 +282,9 @@
     )
 
 
-def head_inner_kernel(block_ref, taps_ref, head_ref, logits_ref, edge_ref, padded):
+def head_inner_kernel(block_ref, taps_ref, head_ref, logits_ref, edge_ref, near_ref, padded):
     rows, width = block_ref.shape
+    near_ref[...] = head_ref[...]
     inner_rows(block_ref, padded)
     keep_edges(block_ref, edge_ref)
     total = jnp.zeros(logits_ref.shape, f32)
@@ -302,9 +303,10 @@
         out_shape=(
             jax.ShapeDtypeStruct((classes, rows), bf16),
             jax.ShapeDtypeStruct((16, width), bf16),
+            jax.ShapeDtypeStruct((classes, width), bf16),
         ),
         in_specs=resident(3),
-        out_specs=tuple(resident(2)),
+        out_specs=tuple(resident(3)),
         scratch_shapes=[pltpu.VMEM((rows + 16, width), f32)],
         cost_estimate=cost(2 * classes * rows * width, 2 * (classes + rows) * width),
         compiler_params=params(8),
@@ -430,8 +432,8 @@
     pre = jnp.dot(got_x, up_one, preferred_element_type=f32)
     hidden = gelu_value(pre).astype(bf16)
     outputs = jnp.dot(hidden, down_one, preferred_element_type=f32).astype(bf16)
+    mix_gates = keep(gates)
     out_slots = exchange(outputs, owners)
-    mix_gates = keep(gates)
 
     back_hidden = jnp.einsum("rd,hd->rh", got_g, down_one, preferred_element_type=f32)
     pre_grad = (back_hidden * gelu_slope(pre)).astype(bf16)
@@ -440,8 +442,9 @@
 
     mixed, gate_grad = mix(target, mix_gates, out_slots, frames, mixed_grad)
     low, high = edges(mixed, margin)
-    inner_logits, edge = head_inner(mixed, smooth_taps, head_t)
-    logits = head_outer(low, edge, high, smooth_taps, head_t, inner_logits)
+    inner_logits, edge, near_head = head_inner(mixed, smooth_taps, head_t)
+    logits = head_outer(low, edge, high, smooth_taps, near_head, inner_logits)
+    gate_grad = keep(gate_grad)
     frame_grad = finish(target, gates, part_slots, mixed_grad)
     return (logits.T, frame_grad, gate_grad.T)
 

time: 127 us -> 128 us (level)
  local copies, waits for them, and re-layouts: 5.93 us -> 11.9 us
  waiting for transfers between devices: 43.2 us -> 40.7 us
  Pallas kernels: 16.2 us -> 14.7 us
  starting transfers between devices: 31.7 us -> 30.2 us
    unnamed x24 -> x30, local copies, waits for them, and re-layouts: 5.15 us -> 11.1 us
    all_to_all x4, waiting for transfers between devices: 43.2 us -> 40.7 us  [exchange(): lax.all_to_all(blocks, 'expert', split_axis=0, concat_axis=0, tiled=True)]
    pallas_call x1, Pallas kernels: 3.21 us -> 0.81 us  [mix(): pl.pallas_call(mix_kernel, out_shape=(jax.ShapeDtypeStruct((rows, width),...]
    all_to_all x4, starting transfers between devices: 23.1 us -> 21.6 us  [exchange(): lax.all_to_all(blocks, 'expert', split_axis=0, concat_axis=0, tiled=True)]
  transfers between devices with their start and end apart: 8 -> 8, of which waited for: 4 -> 4; matrix products, arithmetic and copies ran while one was open for 23% -> 23% of each run, Pallas kernels for 9% -> 8%
where the time goes in v3:
time: 128 us; the launch traced here: 127 us
  waiting for transfers between devices  40.7 us (32%)
  starting transfers between devices  30.2 us (24%)
  matrix products  28.8 us (22%)
  Pallas kernels  14.7 us (11%)
  local copies, waits for them, and re-layouts  11.9 us (9%)
    all_to_all x4, waiting for transfers between devices, exchange(): lax.all_to_all(blocks, 'expert', split_axis=0, concat_axis=0, tiled=True)  40.7 us
    all_to_all x4, starting transfers between devices, exchange(): lax.all_to_all(blocks, 'expert', split_axis=0, concat_axis=0, tiled=True)  21.6 us
    dot_general x1, matrix products, layer(): jnp.einsum('rh,dh->rd', pre_grad, up_one, preferred_element_type=f32)  14.6 us
    unnamed x30, local copies, waits for them, and re-layouts  11.1 us
    dot_general x1, matrix products, layer(): outputs = jnp.dot(hidden, down_one, preferred_element_type=f32).astype(bf16)  7.62 us
    ppermute x2, starting transfers between devices, edges(): low = lax.ppermute(block[block.shape[0] - width:], axes, forward)  6.06 us
    dot_general x1, matrix products, layer(): pre = jnp.dot(got_x, up_one, preferred_element_type=f32)  5.99 us
    pallas_call x1, Pallas kernels, dispatch(): pl.pallas_call(functools.partial(dispatch_kernel, owners, capacity), out_...  2.99 us
  transfers between devices with their start and end apart: 8, of which 4 were waited for; matrix products, arithmetic and copies ran while one was open for 23% of the time, Pallas kernels for 8%

profile of v3, /device:TPU:0, one launch (start us, length us, event | category | flops | bytes accessed | tf_op | source)
XLA Modules:
  0.0 127.2 jit_solution(17165780359726551373)
XLA Ops:
  0.7 3.0 %dispatch.1 = (bf16[512,1536]{1,0:T(8,128)(2,1)}, s32[2,128]{1,0:T(2,128)}) custom-call(s32[2,128]{1,0:T(2,128)} %bitcast.45, bf16[128,1536]{1,0:T(8,128)(2,1)} %frames_ref.3), custom_call_target="tpu_custom_call" | custom-call | flops 201326592 | bytes 1966080 | tf_op jit(solution)/shard_map/dispatch/pallas_call | solution.py:163
  3.7 8.5 %all-to-all-start = ((bf16[32,16,1536]{2,1,0:T(8,128)(2,1)}), bf16[32,16,1536]{2,1,0:T(8,128)(2,1)}, u32[]{:S(2)}, u32[]{:S(2)}) async-start(bf16[32,16,1536]{2,1,0:T(8,128)(2,1)} %bitcast.39), calls=%async_computation | async-start | bytes 3145728 | tf_op jit(solution)/shard_map/all_to_all | solution.py:403
  12.7 1.3 %collective-permute-start.1 = (bf16[4,1536]{1,0:T(4,128)(2,1)S(1)}, bf16[4,1536]{1,0:T(4,128)(2,1)S(1)}, u32[]{:S(2)}, u32[]{:S(2)}) collective-permute-start(bf16[4,1536]{1,0:T(4,128)(2,1)S(1)} %get-tuple-element.27), channel_id=1, source_target_pairs={{1,0},{2,1},{3,2},{4,3},{5,4},{6,5},{7,6},{8,7},{9,8},{10,9},{11,1... | collective-permute-start | bytes 36872 | tf_op jit(solution)/shard_map/ppermute | solution.py:397
  14.0 3.0 %collective-permute-start = (bf16[4,1536]{1,0:T(4,128)(2,1)S(1)}, bf16[4,1536]{1,0:T(4,128)(2,1)S(1)}, u32[]{:S(2)}, u32[]{:S(2)}) collective-permute-start(bf16[4,1536]{1,0:T(4,128)(2,1)S(1)} %get-tuple-element.28), channel_id=1, source_target_pairs={{0,1},{1,2},{2,3},{3,4},{4,5},{5,6},{6,7},{7,8},{8,9},{9,10},{10,1... | collective-permute-start | bytes 36872 | tf_op jit(solution)/shard_map/ppermute | solution.py:396
  18.2 1.8 %grad_dispatch.1 = (bf16[128,1536]{1,0:T(8,128)(2,1)S(1)}, bf16[512,1536]{1,0:T(8,128)(2,1)}) custom-call(s32[2,128]{1,0:T(2,128)S(1)} %copy-done.9, bf16[4,1536]{1,0:T(4,128)(2,1)S(1)} %collective-permute-done.low_ref, bf16[16,1536]{1,0:T(8,128)(2,1)S(1)} %get-tuple-element.16.edge_ref, bf16[4,1536]{1,0:T(4,128)(2,1)S(1)} %collective-permute-done.1.high_ref, ...), custom_call_target="tpu_custom_call" | custom-call | flops 201326592 | bytes 2359296 | tf_op jit(solution)/shard_map/grad_dispatch/pallas_call | solution.py:229
  20.0 16.1 %all-to-all-done = bf16[32,16,1536]{2,1,0:T(8,128)(2,1)} async-done(((bf16[32,16,1536]{2,1,0:T(8,128)(2,1)}), bf16[32,16,1536]{2,1,0:T(8,128)(2,1)}, u32[]{:S(2)}, u32[]{:S(2)}) %all-to-all-start) | async-done | bytes 1572896 | tf_op jit(solution)/shard_map/all_to_all | solution.py:403
  36.1 4.2 %all-to-all-start.2 = ((bf16[32,16,1536]{2,1,0:T(8,128)(2,1)}), bf16[32,16,1536]{2,1,0:T(8,128)(2,1)S(1)}, u32[]{:S(2)}, u32[]{:S(2)}) async-start(bf16[32,16,1536]{2,1,0:T(8,128)(2,1)} %bitcast.10), calls=%async_computation.2 | async-start | bytes 3145728 | tf_op jit(solution)/shard_map/all_to_all | solution.py:403
  40.3 6.0 %fusion.6 = f32[512,2048]{1,0:T(8,128)S(1)} fusion(bf16[512,1536]{1,0:T(8,128)(2,1)} %bitcast.3, bf16[1,1536,2048]{2,1,0:T(8,128)(2,1)} %param.11), kind=kOutput, calls=%fused_computation.6 | convolution fusion | flops 3221225472 | bytes 12058624 | tf_op jit(solution)/shard_map/dot_general | solution.py:432
  46.3 1.9 %copy-done.14 = f32[512,2048]{1,0:T(8,128)} copy-done((f32[512,2048]{1,0:T(8,128)}, f32[512,2048]{1,0:T(8,128)S(1)}, u32[]{:S(2)}) %copy-start.14) | copy-done | bytes 4194328
  48.3 7.6 %fusion.20 = bf16[512,1536]{1,0:T(8,128)(2,1)} fusion(bf16[1,2048,1536]{2,1,0:T(8,128)(2,1)} %param.12, f32[512,2048]{1,0:T(8,128)S(1)} %fusion.6), kind=kOutput, calls=%fused_computation.19 | convolution fusion | flops 3231449088 | bytes 12058624 | tf_op jit(solution)/shard_map/dot_general | solution.py:434
  55.9 8.3 %all-to-all-done.2 = bf16[32,16,1536]{2,1,0:T(8,128)(2,1)S(1)} async-done(((bf16[32,16,1536]{2,1,0:T(8,128)(2,1)}), bf16[32,16,1536]{2,1,0:T(8,128)(2,1)S(1)}, u32[]{:S(2)}, u32[]{:S(2)}) %all-to-all-start.2) | async-done | bytes 1572896 | tf_op jit(solution)/shard_map/all_to_all | solution.py:403
  65.4 4.2 %all-to-all-start.1 = ((bf16[32,16,1536]{2,1,0:T(8,128)(2,1)}), bf16[32,16,1536]{2,1,0:T(8,128)(2,1)S(1)}, u32[]{:S(2)}, u32[]{:S(2)}) async-start(bf16[32,16,1536]{2,1,0:T(8,128)(2,1)} %bitcast.42), calls=%async_computation.1 | async-start | bytes 3145728 | tf_op jit(solution)/shard_map/all_to_all | solution.py:403
  69.6 14.6 %fusion.17 = bf16[512,1536]{1,0:T(8,128)(2,1)} fusion(bf16[1,1536,2048]{2,1,0:T(8,128)(2,1)} %param.11, f32[512,2048]{1,0:T(8,128)} %copy-done.14, bf16[512,1536]{1,0:T(8,128)(2,1)} %bitcast.41, bf16[1,2048,1536]{2,1,0:T(8,128)(2,1)} %param.12), kind=kOutput, calls=%fused_computation.18 | convolution fusion | flops 6463160320 | bytes 19922944 | tf_op jit(solution)/shard_map/rh,dh->rd/dot_general | solution.py:440
  84.2 9.1 %all-to-all-done.1 = bf16[32,16,1536]{2,1,0:T(8,128)(2,1)S(1)} async-done(((bf16[32,16,1536]{2,1,0:T(8,128)(2,1)}), bf16[32,16,1536]{2,1,0:T(8,128)(2,1)S(1)}, u32[]{:S(2)}, u32[]{:S(2)}) %all-to-all-start.1) | async-done | bytes 1572896 | tf_op jit(solution)/shard_map/all_to_all | solution.py:403
  94.5 4.7 %all-to-all-start.3 = ((bf16[32,16,1536]{2,1,0:T(8,128)(2,1)}), bf16[32,16,1536]{2,1,0:T(8,128)(2,1)}, u32[]{:S(2)}, u32[]{:S(2)}) async-start(bf16[32,16,1536]{2,1,0:T(8,128)(2,1)} %bitcast.40), calls=%async_computation.3 | async-start | bytes 3145728 | tf_op jit(solution)/shard_map/all_to_all | solution.py:403
  99.2 1.2 keep.2.gates_ref
  100.4 1.4 %copy-done.4 = bf16[32,16,1536]{2,1,0:T(8,128)(2,1)S(1)} copy-done((bf16[32,16,1536]{2,1,0:T(8,128)(2,1)S(1)}, bf16[32,16,1536]{2,1,0:T(8,128)(2,1)}, u32[]{:S(2)}) %copy-start.4) | copy-done | bytes 1572888
  107.7 1.3 %collective-permute-start.3 = (bf16[4,1536]{1,0:T(4,128)(2,1)S(1)}, bf16[4,1536]{1,0:T(4,128)(2,1)S(1)}, u32[]{:S(2)}, u32[]{:S(2)}) collective-permute-start(bf16[4,1536]{1,0:T(4,128)(2,1)S(1)} %get-tuple-element.25), channel_id=1, source_target_pairs={{1,0},{2,1},{3,2},{4,3},{5,4},{6,5},{7,6},{8,7},{9,8},{10,9},{11,1... | collective-permute-start | bytes 36872 | tf_op jit(solution)/shard_map/ppermute | solution.py:397
  109.0 3.0 %collective-permute-start.2 = (bf16[4,1536]{1,0:T(4,128)(2,1)S(1)}, bf16[4,1536]{1,0:T(4,128)(2,1)S(1)}, u32[]{:S(2)}, u32[]{:S(2)}) collective-permute-start(bf16[4,1536]{1,0:T(4,128)(2,1)S(1)} %get-tuple-element.26), channel_id=1, source_target_pairs={{0,1},{1,2},{2,3},{3,4},{4,5},{5,6},{6,7},{7,8},{8,9},{9,10},{10,1... | collective-permute-start | bytes 36872 | tf_op jit(solution)/shard_map/ppermute | solution.py:396
  112.0 1.4 %copy-done.2 = bf16[1536,527]{0,1:T(8,128)(2,1)S(1)} copy-done((bf16[1536,527]{0,1:T(8,128)(2,1)S(1)}, bf16[1536,527]{0,1:T(8,128)(2,1)}, u32[]{:S(2)}) %copy-start.2) | copy-done | bytes 1618968
  114.4 1.4 %head_inner.1 = (bf16[527,128]{1,0:T(8,128)(2,1)S(1)}, bf16[16,1536]{1,0:T(8,128)(2,1)S(1)}, bf16[527,1536]{1,0:T(8,128)(2,1)S(1)}) custom-call(bf16[128,1536]{1,0:T(8,128)(2,1)S(1)} %copy-done.7, f32[9,1536]{1,0:T(8,128)S(1)} %copy-done.5, bf16[527,1536]{1,0:T(8,128)(2,1)S(1)} %bitcast.35), custom_call_target="tpu_custom_call" | custom-call | flops 207224832 | bytes 2012160 | tf_op jit(solution)/shard_map/head_inner/pallas_call | solution.py:301
  115.8 7.2 %all-to-all-done.3 = bf16[32,16,1536]{2,1,0:T(8,128)(2,1)} async-done(((bf16[32,16,1536]{2,1,0:T(8,128)(2,1)}), bf16[32,16,1536]{2,1,0:T(8,128)(2,1)}, u32[]{:S(2)}, u32[]{:S(2)}) %all-to-all-start.3) | async-done | bytes 1572896 | tf_op jit(solution)/shard_map/all_to_all | solution.py:403
  123.1 2.8 %finish.1 = bf16[128,1536]{1,0:T(8,128)(2,1)} custom-call(s32[2,128]{1,0:T(2,128)S(1)} %copy-done.9, f32[2,128]{1,0:T(2,128)S(1)} %bitcast.38, bf16[512,1536]{1,0:T(8,128)(2,1)} %bitcast.13.slots_ref, bf16[128,1536]{1,0:T(8,128)(2,1)S(1)} %get-tuple-element.18.grad_ref), custom_call_target="tpu_custom_call" | custom-call | flops 402653184 | bytes 2359296 | tf_op jit(solution)/shard_map/finish/pallas_call | solution.py:365
  125.9 1.3 %head_outer.1 = bf16[527,128]{1,0:T(8,128)(2,1)} custom-call(bf16[4,1536]{1,0:T(4,128)(2,1)S(1)} %collective-permute-done.2.low_ref, bf16[16,1536]{1,0:T(8,128)(2,1)S(1)} %get-tuple-element.20.edge_ref, bf16[4,1536]{1,0:T(4,128)(2,1)S(1)} %collective-permute-done.3.high_ref, f32[9,1536]{1,0:T(8,128)S(1)} %copy-done.5, ...), custom_call_target="tpu_custom_call" | custom-call | flops 207224832 | bytes 2012160 | tf_op jit(solution)/shard_map/head_outer/pallas_call | solution.py:337
  (37 shorter events, 10.8 us)
Async XLA Ops:
  0.6 11.6 %copy-start = (bf16[128,527]{0,1:T(8,128)(2,1)S(1)}, bf16[128,527]{0,1:T(8,128)(2,1)}, u32[]{:S(2)}) copy-start(bf16[128,527]{0,1:T(8,128)(2,1)} %param.15) | copy-start | bytes 404740
  0.6 11.5 %copy-start.1 = (bf16[1536,527]{0,1:T(8,128)(2,1)S(1)}, bf16[1536,527]{0,1:T(8,128)(2,1)}, u32[]{:S(2)}) copy-start(bf16[1536,527]{0,1:T(8,128)(2,1)} %param.14) | copy-start | bytes 4856836
  0.7 16.4 %copy-start.5 = (f32[9,1536]{1,0:T(8,128)S(1)}, f32[9,1536]{1,0:T(8,128)}, u32[]{:S(2)}) copy-start(f32[9,1536]{1,0:T(8,128)} %taps_ref.7) | copy-start | bytes 165892
  3.7 14.5 %copy-start.9 = (s32[2,128]{1,0:T(2,128)S(1)}, s32[2,128]{1,0:T(2,128)}, u32[]{:S(2)}) copy-start(s32[2,128]{1,0:T(2,128)} %get-tuple-element.14.target_ref) | copy-start | bytes 3076
  3.7 32.4 %all-to-all-start = ((bf16[32,16,1536]{2,1,0:T(8,128)(2,1)}), bf16[32,16,1536]{2,1,0:T(8,128)(2,1)}, u32[]{:S(2)}, u32[]{:S(2)}) async-start(bf16[32,16,1536]{2,1,0:T(8,128)(2,1)} %bitcast.39), calls=%async_computation | async-start | bytes 3145728 | tf_op jit(solution)/shard_map/all_to_all | solution.py:403
  12.7 5.4 %collective-permute-start.1 = (bf16[4,1536]{1,0:T(4,128)(2,1)S(1)}, bf16[4,1536]{1,0:T(4,128)(2,1)S(1)}, u32[]{:S(2)}, u32[]{:S(2)}) collective-permute-start(bf16[4,1536]{1,0:T(4,128)(2,1)S(1)} %get-tuple-element.27), channel_id=1, source_target_pairs={{1,0},{2,1},{3,2},{4,3},{5,4},{6,5},{7,6},{8,7},{9,8},{10,9},{11,1... | collective-permute-start | bytes 36872 | tf_op jit(solution)/shard_map/ppermute | solution.py:397
  14.0 4.1 %collective-permute-start = (bf16[4,1536]{1,0:T(4,128)(2,1)S(1)}, bf16[4,1536]{1,0:T(4,128)(2,1)S(1)}, u32[]{:S(2)}, u32[]{:S(2)}) collective-permute-start(bf16[4,1536]{1,0:T(4,128)(2,1)S(1)} %get-tuple-element.28), channel_id=1, source_target_pairs={{0,1},{1,2},{2,3},{3,4},{4,5},{5,6},{6,7},{7,8},{8,9},{9,10},{10,1... | collective-permute-start | bytes 36872 | tf_op jit(solution)/shard_map/ppermute | solution.py:396
  36.1 28.1 %all-to-all-start.2 = ((bf16[32,16,1536]{2,1,0:T(8,128)(2,1)}), bf16[32,16,1536]{2,1,0:T(8,128)(2,1)S(1)}, u32[]{:S(2)}, u32[]{:S(2)}) async-start(bf16[32,16,1536]{2,1,0:T(8,128)(2,1)} %bitcast.10), calls=%async_computation.2 | async-start | bytes 3145728 | tf_op jit(solution)/shard_map/all_to_all | solution.py:403
  46.3 2.0 %copy-start.14 = (f32[512,2048]{1,0:T(8,128)}, f32[512,2048]{1,0:T(8,128)S(1)}, u32[]{:S(2)}) copy-start(f32[512,2048]{1,0:T(8,128)S(1)} %fusion.6) | copy-start | bytes 12582916
  64.2 1.2 copy-start.13
  65.4 27.9 %all-to-all-start.1 = ((bf16[32,16,1536]{2,1,0:T(8,128)(2,1)}), bf16[32,16,1536]{2,1,0:T(8,128)(2,1)S(1)}, u32[]{:S(2)}, u32[]{:S(2)}) async-start(bf16[32,16,1536]{2,1,0:T(8,128)(2,1)} %bitcast.42), calls=%async_computation.1 | async-start | bytes 3145728 | tf_op jit(solution)/shard_map/all_to_all | solution.py:403
  84.2 38.8 %copy-start.10 = (f32[128,2]{0,1:T(2,128)S(1)}, f32[128,2]{0,1:T(2,128)}, u32[]{:S(2)}) copy-start(f32[128,2]{0,1:T(2,128)} %param.10) | copy-start | bytes 3076
  93.3 1.1 copy-start.3
  94.5 28.6 %all-to-all-start.3 = ((bf16[32,16,1536]{2,1,0:T(8,128)(2,1)}), bf16[32,16,1536]{2,1,0:T(8,128)(2,1)}, u32[]{:S(2)}, u32[]{:S(2)}) async-start(bf16[32,16,1536]{2,1,0:T(8,128)(2,1)} %bitcast.40), calls=%async_computation.3 | async-start | bytes 3145728 | tf_op jit(solution)/shard_map/all_to_all | solution.py:403
  100.4 1.4 %copy-start.4 = (bf16[32,16,1536]{2,1,0:T(8,128)(2,1)S(1)}, bf16[32,16,1536]{2,1,0:T(8,128)(2,1)}, u32[]{:S(2)}) copy-start(bf16[32,16,1536]{2,1,0:T(8,128)(2,1)} %copy-done.3) | copy-start | bytes 4718596
  101.8 1.0 copy-start.8
  102.8 0.7 copy-start.11
  104.3 0.7 copy-start.6
  105.1 0.6 copy-start.12
  107.7 18.3 %collective-permute-start.3 = (bf16[4,1536]{1,0:T(4,128)(2,1)S(1)}, bf16[4,1536]{1,0:T(4,128)(2,1)S(1)}, u32[]{:S(2)}, u32[]{:S(2)}) collective-permute-start(bf16[4,1536]{1,0:T(4,128)(2,1)S(1)} %get-tuple-element.25), channel_id=1, source_target_pairs={{1,0},{2,1},{3,2},{4,3},{5,4},{6,5},{7,6},{8,7},{9,8},{10,9},{11,1... | collective-permute-start | bytes 36872 | tf_op jit(solution)/shard_map/ppermute | solution.py:397
  109.0 17.0 %collective-permute-start.2 = (bf16[4,1536]{1,0:T(4,128)(2,1)S(1)}, bf16[4,1536]{1,0:T(4,128)(2,1)S(1)}, u32[]{:S(2)}, u32[]{:S(2)}) collective-permute-start(bf16[4,1536]{1,0:T(4,128)(2,1)S(1)} %get-tuple-element.26), channel_id=1, source_target_pairs={{0,1},{1,2},{2,3},{3,4},{4,5},{5,6},{6,7},{7,8},{8,9},{9,10},{10,1... | collective-permute-start | bytes 36872 | tf_op jit(solution)/shard_map/ppermute | solution.py:396
  112.0 1.4 %copy-start.2 = (bf16[1536,527]{0,1:T(8,128)(2,1)S(1)}, bf16[1536,527]{0,1:T(8,128)(2,1)}, u32[]{:S(2)}) copy-start(bf16[1536,527]{0,1:T(8,128)(2,1)} %param.14) | copy-start | bytes 4856836
  113.4 1.0 copy-start.7
